TPU v7x, 256 devices: a whole 4x4x8 slice. The times are simulated.
256 devices in a mesh: gx: 32 (over x, z), gy: 8 (over y, core).
Axes of the slice: x: 4, y: 4, z: 8, core: 2. Of those that a mesh axis runs over, the one named last changes fastest.
Arguments:
- depth: float32 [4096, 4096], P('gx', 'gy'), may hold values from 0.3 to 1.2
- momentum_x: float32 [4096, 4096], P('gx', 'gy'), may hold values from -3 to 3
- momentum_y: float32 [4096, 4096], P('gx', 'gy'), may hold values from -3 to 3
- bed: float32 [4096, 4096], P('gx', 'gy'), may hold values from -1 to 1
- wet: int32 [4096, 4096], P('gx', 'gy'), may hold values 0 or 1
Outputs:
- new_depth: float32 [4096, 4096], P('gx', 'gy')
- velocity_x: float32 [4096, 4096], P('gx', 'gy')
- velocity_y: float32 [4096, 4096], P('gx', 'gy')
All inputs are finite; a program needn't handle non-finite values. No bound on the sum of `wet` on one device may be relied on, other than what follows from the above.
Results may differ from a plain program's by a relative error of at most 0.0013.
Values sent between devices are 32-bit elements; how exact they have to be, the bound alone decides.
A program may use at most 64 MiB of HBM per device.

v0:
```python
import jax
import jax.numpy as jnp
from jax import lax
from jax.sharding import PartitionSpec as P

gravity = 9.81
ratio_x = 0.05
ratio_y = 0.05


def with_halo(block, sides, width):
    for axis, dim in sides:
        count = lax.axis_size(axis)
        forward = [(i, i + 1) for i in range(count - 1)]
        backward = [(target, source) for source, target in forward]
        low = lax.ppermute(
            lax.slice_in_dim(block, block.shape[dim] - width, None, axis=dim), axis, forward
        )
        high = lax.ppermute(lax.slice_in_dim(block, 0, width, axis=dim), axis, backward)
        block = jnp.concatenate([low, block, high], axis=dim)
    return block


def minmod(left, right):
    return 0.5 * (jnp.sign(left) + jnp.sign(right)) * jnp.minimum(jnp.abs(left), jnp.abs(right))


def window(values, start, stop, line_axis):
    return lax.slice_in_dim(values, start, stop, axis=line_axis)


def physical(height, normal, across):
    speed_n = normal / height
    fluxes = (normal, normal * speed_n + 0.5 * gravity * height * height, across * speed_n)
    return (fluxes, jnp.abs(speed_n) + jnp.sqrt(gravity * height))


def face_terms(depth, normal, across, wet_cells, line_axis):
    length = depth.shape[line_axis]
    states = (depth, normal, across)
    slopes = [
        minmod(
            window(field, 1, length - 1, line_axis) - window(field, 0, length - 2, line_axis),
            window(field, 2, length, line_axis) - window(field, 1, length - 1, line_axis),
        )
        for field in states
    ]
    lefts = [
        window(field, 1, length - 2, line_axis) + 0.5 * window(slope, 0, length - 3, line_axis)
        for field, slope in zip(states, slopes)
    ]
    rights = [
        window(field, 2, length - 1, line_axis) - 0.5 * window(slope, 1, length - 2, line_axis)
        for field, slope in zip(states, slopes)
    ]
    opened = window(wet_cells, 1, length - 2, line_axis) * window(
        wet_cells, 2, length - 1, line_axis
    )
    safe_left = jnp.where(opened > 0.5, lefts[0], 1.0)
    safe_right = jnp.where(opened > 0.5, rights[0], 1.0)
    flux_left, speed_left = physical(safe_left, lefts[1], lefts[2])
    flux_right, speed_right = physical(safe_right, rights[1], rights[2])
    fastest = jnp.maximum(speed_left, speed_right)
    result = []
    for flux_a, flux_b, state_a, state_b in zip(flux_left, flux_right, lefts, rights):
        face = opened * (0.5 * (flux_a + flux_b) - 0.5 * fastest * (state_b - state_a))
        count = face.shape[line_axis]
        result.append(window(face, 1, count, line_axis) - window(face, 0, count - 1, line_axis))
    return result


def predict(padded):
    along_x = padded[:, :, 2:-2]
    along_y = padded[:, 2:-2, :]
    center = padded[:, 2:-2, 2:-2]
    depth, flow_x, flow_y, wet_cells = (center[0], center[1], center[2], center[4])
    mass_x, normal_x, shear_x = face_terms(along_x[0], along_x[1], along_x[2], along_x[4], 0)
    mass_y, normal_y, shear_y = face_terms(along_y[0], along_y[2], along_y[1], along_y[4], 1)
    bed_x = 0.5 * (along_x[3, 3:-1] - along_x[3, 1:-3])
    bed_y = 0.5 * (along_y[3, :, 3:-1] - along_y[3, :, 1:-3])
    new_depth = depth - wet_cells * (ratio_x * mass_x + ratio_y * mass_y)
    push_x = wet_cells * (
        flow_x - ratio_x * normal_x - ratio_y * shear_y - ratio_x * gravity * depth * bed_x
    )
    push_y = wet_cells * (
        flow_y - ratio_x * shear_x - ratio_y * normal_y - ratio_y * gravity * depth * bed_y
    )
    return (new_depth, push_x, push_y)


def earlier(values, stride, line_axis, fill):
    which = line_axis % values.ndim
    widths = [(0, 0)] * values.ndim
    widths[which] = (stride, 0)
    padded = jnp.pad(values, widths, constant_values=fill)
    return lax.slice_in_dim(padded, 0, values.shape[which], axis=which)


def later(values, stride, line_axis, fill):
    which = line_axis % values.ndim
    widths = [(0, 0)] * values.ndim
    widths[which] = (0, stride)
    padded = jnp.pad(values, widths, constant_values=fill)
    return lax.slice_in_dim(padded, stride, stride + values.shape[which], axis=which)


def eliminate(rows, below, above):
    lower, diagonal, upper, right = rows
    left_factor = lower / below[1]
    right_factor = upper / above[1]
    return (
        -left_factor * below[0],
        diagonal - left_factor * below[2] - right_factor * above[0],
        -right_factor * above[2],
        right - left_factor * below[3] - right_factor * above[3],
    )


def reduce_lines(lower, diagonal, upper, right, line_axis):
    count = diagonal.shape[line_axis % diagonal.ndim]
    rows = (lower, diagonal, upper, right)
    stride = 1
    while stride < count:
        below = tuple(
            (
                earlier(member, stride, line_axis, fill)
                for member, fill in zip(rows, (0.0, 1.0, 0.0, 0.0))
            )
        )
        above = tuple(
            (
                later(member, stride, line_axis, fill)
                for member, fill in zip(rows, (0.0, 1.0, 0.0, 0.0))
            )
        )
        rows = lax.optimization_barrier(eliminate(rows, below, above))
        stride *= 2
    return rows[3] / rows[1]


def separator_rows(last_six, next_three):
    solved_y, solved_g, solved_e, sep_coef, sep_diag, sep_right = last_six
    first_y, first_g, first_e = next_three
    return (
        -sep_coef * solved_g,
        sep_diag - sep_coef * solved_e - sep_coef * first_g,
        -sep_coef * first_e,
        sep_right + sep_coef * solved_y + sep_coef * first_y,
    )


def local_spikes(coefficient, right, line_axis):
    which = line_axis % 2
    count = coefficient.shape[which]
    inner = lax.slice_in_dim(coefficient, 0, count - 1, axis=which)
    position = lax.broadcasted_iota(jnp.int32, inner.shape, which)
    zeros = jnp.zeros_like(inner)
    sources = jnp.stack(
        [
            lax.slice_in_dim(right, 0, count - 1, axis=which),
            jnp.where(position == 0, inner, zeros),
            jnp.where(position == count - 2, inner, zeros),
        ]
    )
    solved = reduce_lines(-inner, 1.0 + 2.0 * inner, -inner, sources, line_axis)
    first = lax.index_in_dim(solved, 0, which + 1, keepdims=False)
    final = lax.index_in_dim(solved, count - 2, which + 1, keepdims=False)
    sep_coef = lax.index_in_dim(coefficient, count - 1, which, keepdims=False)
    sep_right = lax.index_in_dim(right, count - 1, which, keepdims=False)
    last_six = jnp.concatenate([final, jnp.stack([sep_coef, 1.0 + 2.0 * sep_coef, sep_right])])
    return (solved, first, last_six)


def assemble(solved, own, previous, line_axis):
    which = line_axis % 2
    own_wide = jnp.expand_dims(own, which)
    prev_wide = jnp.expand_dims(previous, which)
    inner = solved[0] + solved[1] * prev_wide + solved[2] * own_wide
    return jnp.concatenate([inner, own_wide], axis=which)


def pick_rows(whole, index):
    first_all = whole[:3]
    rows = separator_rows(whole[3:], later(first_all, 1, -2, 0.0))
    solved = reduce_lines(rows[0], rows[1], rows[2], rows[3], -2)
    own = lax.dynamic_index_in_dim(solved, index, 0, keepdims=False)
    previous = lax.dynamic_index_in_dim(earlier(solved, 1, -2, 0.0), index, 0, keepdims=False)
    return (own, previous)


def interface_x(first, last_six):
    packed = jnp.concatenate([first, last_six])[:, None, :]
    whole = lax.all_gather(packed, "gx", axis=1, tiled=True)
    return pick_rows(whole, lax.axis_index("gx"))


def interface_y(first, last_six):
    packed = jnp.concatenate([first, last_six])[:, None, :]
    whole = lax.all_gather(packed, "gy", axis=1, tiled=True)
    return pick_rows(whole, lax.axis_index("gy"))


def on_device(depth, momentum_x, momentum_y, bed, wet):
    stacked = jnp.stack([depth, momentum_x, momentum_y, bed, wet.astype(jnp.float32)])
    padded = with_halo(stacked, (("gx", 1), ("gy", 2)), 2)
    new_depth, push_x, push_y = predict(padded)
    cells_x = depth.shape[0] * lax.axis_size("gx")
    cells_y = depth.shape[1] * lax.axis_size("gy")
    scale_x = (cells_x / 4.0) ** 2 / 3.0
    scale_y = (cells_y / 4.0) ** 2 / 3.0
    coef_x = scale_x * depth * depth
    coef_y = scale_y * depth * depth
    solved_x, first_x, last_x = local_spikes(coef_x, push_x, -2)
    own_x, prev_x = interface_x(first_x, last_x)
    flux_u = assemble(solved_x, own_x, prev_x, -2)
    solved_y, first_y, last_y = local_spikes(coef_y, push_y, -1)
    own_y, prev_y = interface_y(first_y, last_y)
    flux_v = assemble(solved_y, own_y, prev_y, -1)
    return (new_depth, flux_u / depth, flux_v / depth)


def solution(mesh):
    placed = (P("gx", "gy"), P("gx", "gy"), P("gx", "gy"), P("gx", "gy"), P("gx", "gy"))
    return jax.shard_map(
        on_device,
        mesh=mesh,
        in_specs=placed,
        out_specs=(P("gx", "gy"), P("gx", "gy"), P("gx", "gy")),
        check_vma=False,
    )
```

profile of v0, /device:TPU:8, one launch (start us, length us, event | category | flops | bytes accessed | tf_op | source)
XLA Modules:
  0.0 121.2 jit_solution(9153613067700028402)
XLA Ops:
  0.7 1.0 bitcast_dynamic-update-slice_fusion.4
  1.7 1.0 bitcast_dynamic-update-slice_fusion.3
  2.7 1.0 bitcast_dynamic-update-slice_fusion.2
  3.7 3.8 %collective-permute-start = (f32[5,2,512]{2,1,0:T(2,128)S(1)}, f32[5,2,512]{2,1,0:T(2,128)S(1)}, u32[]{:S(2)}, u32[]{:S(2)}) collective-permute-start(f32[5,2,512]{2,1,0:T(2,128)S(1)} %get-tuple-element.274), channel_id=1, source_target_pairs={{0,8},{8,16},{16,24},{24,32},{32,40},{40,48},{48,56},{56,64},{64,7... | collective-permute-start | bytes 61448 | tf_op jit(solution)/shard_map/ppermute | solution.py:16
  7.6 1.3 %collective-permute-start.1 = (f32[5,2,512]{2,1,0:T(2,128)S(1)}, f32[5,2,512]{2,1,0:T(2,128)S(1)}, u32[]{:S(2)}, u32[]{:S(2)}) collective-permute-start(f32[5,2,512]{2,1,0:T(2,128)S(1)} %get-tuple-element.275), channel_id=1, source_target_pairs={{8,0},{16,8},{24,16},{32,24},{40,32},{48,40},{56,48},{64,56},{72,6... | collective-permute-start | bytes 61448 | tf_op jit(solution)/shard_map/ppermute | solution.py:19
  8.9 0.6 iota_compare_fusion.2
  9.5 3.8 %collective-permute-done.1 = f32[5,2,512]{2,1,0:T(2,128)S(1)} collective-permute-done((f32[5,2,512]{2,1,0:T(2,128)S(1)}, f32[5,2,512]{2,1,0:T(2,128)S(1)}, u32[]{:S(2)}, u32[]{:S(2)}) %collective-permute-start.1) | collective-permute-done | bytes 20512 | tf_op jit(solution)/shard_map/ppermute | solution.py:19
  13.7 1.9 %collective-permute-start.2 = (f32[5,132,2]{2,1,0:T(8,128)S(1)}, f32[5,132,2]{2,1,0:T(8,128)S(1)}, u32[]{:S(2)}, u32[]{:S(2)}) collective-permute-start(f32[5,132,2]{2,1,0:T(8,128)S(1)} %get-tuple-element.272), channel_id=1, source_target_pairs={{0,1},{1,2},{2,3},{3,4},{4,5},{5,6},{6,7},{8,9},{9,10},{10,11},{11... | collective-permute-start | bytes 15848 | tf_op jit(solution)/shard_map/ppermute | solution.py:16
  15.6 3.6 %collective-permute-start.3 = (f32[5,132,2]{2,1,0:T(8,128)S(1)}, f32[5,132,2]{2,1,0:T(8,128)S(1)}, u32[]{:S(2)}, u32[]{:S(2)}) collective-permute-start(f32[5,132,2]{2,1,0:T(8,128)S(1)} %get-tuple-element.273), channel_id=1, source_target_pairs={{1,0},{2,1},{3,2},{4,3},{5,4},{6,5},{7,6},{9,8},{10,9},{11,10},{12... | collective-permute-start | bytes 15848 | tf_op jit(solution)/shard_map/ppermute | solution.py:19
  19.3 1.5 %minimum_multiply_fusion.4 = (f32[1,130,512]{2,1,0:T(8,128)S(1)}, f32[1,130,512]{2,1,0:T(8,128)S(1)}, f32[1,130,512]{2,1,0:T(8,128)S(1)}) fusion(f32[5,2,512]{2,1,0:T(2,128)} %copy-done.15, f32[5,128,512]{2,1,0:T(8,128)S(1)} %bitcast_dynamic-update-slice_fusion, f32[5,2,512]{2,1,0:T(2,128)} %copy-done.12, f32[5,132,512]{2,1,0:T(8,128)S(1)} %pad_maximum_fusion), kind=kLoop, calls=%fused_computation.293 | loop fusion | flops 2396160 | bytes 2949120 | tf_op jit(solution)/shard_map/mul | solution.py:25
  20.8 0.6 subtract_multiply_fusion.2
  21.4 1.2 fusion.73
  22.5 1.5 %collective-permute-done.3 = f32[5,132,2]{2,1,0:T(8,128)S(1)} collective-permute-done((f32[5,132,2]{2,1,0:T(8,128)S(1)}, f32[5,132,2]{2,1,0:T(8,128)S(1)}, u32[]{:S(2)}, u32[]{:S(2)}) %collective-permute-start.3) | collective-permute-done | bytes 5312 | tf_op jit(solution)/shard_map/ppermute | solution.py:19
  24.0 0.4 fusion.64
  24.4 0.3 minimum_multiply_fusion.2
  24.8 1.3 %minimum_multiply_fusion = (f32[128,514]{1,0:T(8,128)}, f32[128,514]{1,0:T(8,128)S(1)}) fusion(f32[128,516]{1,0:T(8,128)S(1)} %get-tuple-element.267, f32[128,516]{1,0:T(8,128)S(1)} %get-tuple-element.268), kind=kLoop, calls=%fused_computation.214 | loop fusion | flops 1315840 | bytes 2105344 | tf_op jit(solution)/shard_map/mul | solution.py:25
  26.2 0.8 subtract_multiply_fusion.1
  27.0 0.8 fusion.60
  28.1 1.1 fusion.232
  29.5 0.7 slice_reduce_fusion.2
  30.4 0.3 multiply_subtract_fusion.2
  30.9 0.5 multiply_subtract_fusion
  31.6 0.3 fusion.151
  32.0 0.5 fusion.22
  32.7 0.3 fusion.159
  33.2 0.5 fusion.26
  33.9 0.3 fusion.167
  34.3 0.5 fusion.30
  35.0 0.3 fusion.175
  35.4 0.5 fusion.34
  36.1 0.3 fusion.183
  36.5 0.5 fusion.38
  37.2 0.3 fusion.191
  37.5 0.3 fusion.188
  37.8 0.5 fusion.42
  39.0 0.9 copy-done
  39.9 0.3 slice_reduce_fusion
  40.2 0.5 multiply_add_fusion.3
  40.7 1.3 %concatenate.52 = f32[9,128]{1,0:T(8,128)S(1)} concatenate(f32[3,128]{1,0:T(4,128)S(1)} %get-tuple-element.189, f32[3,128]{1,0:T(4,128)S(1)} %get-tuple-element.188, f32[1,128]{1,0:T(1,128)} %bitcast.173, f32[1,128]{1,0:T(1,128)} %multiply_add_fusion.3, f32[1,128]{1,0:T(1,128)} %bitcast.174), dimensions={0} | concatenate | bytes 9216 | tf_op jit(solution)/shard_map/concatenate | solution.py:198
  42.0 13.1 %all-gather.1 = f32[9,1024]{1,0:T(8,128)S(1)} all-gather(f32[9,128]{1,0:T(8,128)S(1)} %concatenate.52), channel_id=3, replica_groups=mesh['gx'=32,'gy'=8] {'gy'}, dimensions={1}, use_global_device_ids=true | all-gather | bytes 41472 | tf_op jit(solution)/shard_map/all_gather | solution.py:199
  55.1 0.9 multiply_add_fusion.1
  56.0 1.8 %subtract_multiply_fusion = f32[128,513]{1,0:T(8,128)} fusion(f32[128,514]{1,0:T(8,128)S(1)} %copy-done.4, f32[128,516]{1,0:T(8,128)S(1)} %get-tuple-element.267, f32[128,516]{1,0:T(8,128)S(1)} %maximum_bitcast_fusion.2, f32[128,514]{1,0:T(8,128)S(1)} %minimum_multiply_fusion.2, f32[128,516]{1,0:T(8,128)S(1)} %get-tuple-element.269, ...), kind=kLoop, calls=%fused_computation.213 | loop fusion | flops 2232576 | bytes 3939840 | tf_op jit(solution)/shard_map/mul | solution.py:66
  58.0 0.7 copy.28
  58.7 1.2 fusion.224
  60.0 2.0 %maximum_divide_fusion.1 = (f32[128,512]{1,0:T(8,128)}, f32[128,512]{1,0:T(8,128)S(1)}) fusion(f32[128,512]{1,0:T(8,128)S(1)} %copy-done.3, f32[128,1]{1,0:T(8,128)} %copy.28, f32[128,511]{1,0:T(8,128)S(1)} %fusion.224, f32[5,128,512]{2,1,0:T(8,128)S(1)} %bitcast_dynamic-update-slice_fusion, f32[5,2,512]{2,1,0:T(2,128)S(1)} %copy-done.14, ...), kind=kLoop, calls=%fused_computation.461 | loop fusion | flops 1114112 | bytes 3973120 | tf_op jit(solution)/shard_map/div | solution.py:219
  65.2 53.4 %all-gather = f32[9,16384]{1,0:T(8,128)S(1)} all-gather(f32[9,512]{1,0:T(8,128)S(1)} %concatenate.48), channel_id=2, replica_groups=mesh['gx'=32,'gy'=8] {'gx'}, dimensions={1}, use_global_device_ids=true | all-gather | bytes 608256 | tf_op jit(solution)/shard_map/all_gather | solution.py:193
  118.6 1.0 slice_reduce_fusion.4
  120.5 0.7 maximum_divide_fusion
  (143 shorter events, 8.1 us)
Async XLA Ops:
  0.6 3.0 %copy-start.18 = (f32[128,512]{1,0:T(8,128)S(1)}, f32[128,512]{1,0:T(8,128)}, u32[]{:S(2)}) copy-start(f32[128,512]{1,0:T(8,128)} %param.8) | copy-start | bytes 786436
  0.6 3.0 %copy-start.6 = (s32[128,512]{1,0:T(8,128)S(1)}, s32[128,512]{1,0:T(8,128)}, u32[]{:S(2)}) copy-start(s32[128,512]{1,0:T(8,128)} %param.9) | copy-start | bytes 786436
  3.7 5.7 %collective-permute-start = (f32[5,2,512]{2,1,0:T(2,128)S(1)}, f32[5,2,512]{2,1,0:T(2,128)S(1)}, u32[]{:S(2)}, u32[]{:S(2)}) collective-permute-start(f32[5,2,512]{2,1,0:T(2,128)S(1)} %get-tuple-element.274), channel_id=1, source_target_pairs={{0,8},{8,16},{16,24},{24,32},{32,40},{40,48},{48,56},{56,64},{64,7... | collective-permute-start | bytes 61448 | tf_op jit(solution)/shard_map/ppermute | solution.py:16
  7.6 5.7 %collective-permute-start.1 = (f32[5,2,512]{2,1,0:T(2,128)S(1)}, f32[5,2,512]{2,1,0:T(2,128)S(1)}, u32[]{:S(2)}, u32[]{:S(2)}) collective-permute-start(f32[5,2,512]{2,1,0:T(2,128)S(1)} %get-tuple-element.275), channel_id=1, source_target_pairs={{8,0},{16,8},{24,16},{32,24},{40,32},{48,40},{56,48},{64,56},{72,6... | collective-permute-start | bytes 61448 | tf_op jit(solution)/shard_map/ppermute | solution.py:19
  9.5 6.1 %copy-start.12 = (f32[5,2,512]{2,1,0:T(2,128)}, f32[5,2,512]{2,1,0:T(2,128)S(1)}, u32[]{:S(2)}) copy-start(f32[5,2,512]{2,1,0:T(2,128)S(1)} %collective-permute-done) | copy-start | bytes 61444
  13.2 2.4 %copy-start.15 = (f32[5,2,512]{2,1,0:T(2,128)}, f32[5,2,512]{2,1,0:T(2,128)S(1)}, u32[]{:S(2)}) copy-start(f32[5,2,512]{2,1,0:T(2,128)S(1)} %collective-permute-done.1) | copy-start | bytes 61444
  13.7 8.9 %collective-permute-start.2 = (f32[5,132,2]{2,1,0:T(8,128)S(1)}, f32[5,132,2]{2,1,0:T(8,128)S(1)}, u32[]{:S(2)}, u32[]{:S(2)}) collective-permute-start(f32[5,132,2]{2,1,0:T(8,128)S(1)} %get-tuple-element.272), channel_id=1, source_target_pairs={{0,1},{1,2},{2,3},{3,4},{4,5},{5,6},{6,7},{8,9},{9,10},{10,11},{11... | collective-permute-start | bytes 15848 | tf_op jit(solution)/shard_map/ppermute | solution.py:16
  15.6 8.4 %collective-permute-start.3 = (f32[5,132,2]{2,1,0:T(8,128)S(1)}, f32[5,132,2]{2,1,0:T(8,128)S(1)}, u32[]{:S(2)}, u32[]{:S(2)}) collective-permute-start(f32[5,132,2]{2,1,0:T(8,128)S(1)} %get-tuple-element.273), channel_id=1, source_target_pairs={{1,0},{2,1},{3,2},{4,3},{5,4},{6,5},{7,6},{9,8},{10,9},{11,10},{12... | collective-permute-start | bytes 15848 | tf_op jit(solution)/shard_map/ppermute | solution.py:19
  19.3 1.5 %copy-start.13 = (f32[5,2,512]{2,1,0:T(2,128)S(1)}, f32[5,2,512]{2,1,0:T(2,128)}, u32[]{:S(2)}) copy-start(f32[5,2,512]{2,1,0:T(2,128)} %copy-done.12) | copy-start | bytes 61444
  19.3 1.5 %copy-start.16 = (f32[5,2,512]{2,1,0:T(2,128)S(1)}, f32[5,2,512]{2,1,0:T(2,128)}, u32[]{:S(2)}) copy-start(f32[5,2,512]{2,1,0:T(2,128)} %copy-done.15) | copy-start | bytes 61444
  27.0 1.0 copy-start.2
  27.0 1.0 copy-start.7
  27.0 1.1 copy-start.11
  29.4 10.8 %copy-start.19 = (f32[128]{0:T(128)}, f32[128]{0:T(128)S(1)}, u32[]{:S(2)}) copy-start(f32[128]{0:T(128)S(1)} %slice_reduce_fusion.3) | copy-start | bytes 1540
  39.0 0.9 copy-start
  42.0 14.0 %copy-start.4 = (f32[128,514]{1,0:T(8,128)S(1)}, f32[128,514]{1,0:T(8,128)}, u32[]{:S(2)}) copy-start(f32[128,514]{1,0:T(8,128)} %get-tuple-element.331) | copy-start | bytes 789508
  57.8 2.1 %copy-start.3 = (f32[128,512]{1,0:T(8,128)S(1)}, f32[128,512]{1,0:T(8,128)}, u32[]{:S(2)}) copy-start(f32[128,512]{1,0:T(8,128)} %param.5) | copy-start | bytes 786436
  57.8 2.2 %copy-start.8 = (s32[128,512]{1,0:T(8,128)S(1)}, s32[128,512]{1,0:T(8,128)}, u32[]{:S(2)}) copy-start(s32[128,512]{1,0:T(8,128)} %param.9) | copy-start | bytes 786436
  57.8 2.2 %copy-start.9 = (f32[129,512]{1,0:T(8,128)S(1)}, f32[129,512]{1,0:T(8,128)}, u32[]{:S(2)}) copy-start(f32[129,512]{1,0:T(8,128)} %get-tuple-element.270) | copy-start | bytes 792580
  57.8 2.2 %copy-start.10 = (f32[128,513]{1,0:T(8,128)S(1)}, f32[128,513]{1,0:T(8,128)}, u32[]{:S(2)}) copy-start(f32[128,513]{1,0:T(8,128)} %subtract_multiply_fusion) | copy-start | bytes 787972
  57.8 2.2 %copy-start.14 = (f32[5,2,512]{2,1,0:T(2,128)S(1)}, f32[5,2,512]{2,1,0:T(2,128)}, u32[]{:S(2)}) copy-start(f32[5,2,512]{2,1,0:T(2,128)} %copy-done.12) | copy-start | bytes 61444
  57.8 2.2 %copy-start.17 = (f32[5,2,512]{2,1,0:T(2,128)S(1)}, f32[5,2,512]{2,1,0:T(2,128)}, u32[]{:S(2)}) copy-start(f32[5,2,512]{2,1,0:T(2,128)} %copy-done.15) | copy-start | bytes 61444
  60.0 2.1 %copy-start.1 = (f32[127,512]{1,0:T(8,128)S(1)}, f32[127,512]{1,0:T(8,128)}, u32[]{:S(2)}) copy-start(f32[127,512]{1,0:T(8,128)} %get-tuple-element.294) | copy-start | bytes 780292
  60.0 2.1 %copy-start.5 = (f32[127,512]{1,0:T(8,128)S(1)}, f32[127,512]{1,0:T(8,128)}, u32[]{:S(2)}) copy-start(f32[127,512]{1,0:T(8,128)} %get-tuple-element.293) | copy-start | bytes 780292
  60.0 2.1 %copy-start.20 = (pred[127]{0:T(512)(128)(4,1)S(1)}, pred[127]{0:T(512)(128)(4,1)}, u32[]{:S(2)}) copy-start(pred[127]{0:T(512)(128)(4,1)} %get-tuple-element.333) | copy-start | bytes 385
  60.0 2.1 %copy-start.21 = (pred[127]{0:T(512)(128)(4,1)S(1)}, pred[127]{0:T(512)(128)(4,1)}, u32[]{:S(2)}) copy-start(pred[127]{0:T(512)(128)(4,1)} %get-tuple-element.334) | copy-start | bytes 385
where the time goes:
time: 122 us; the launch traced here: 121 us
  blocking collectives  66.5 us (55%)
  other arithmetic  28 us (23%)
  starting transfers between devices  10.7 us (9%)
  local copies, waits for them, and re-layouts  9.07 us (7%)
  waiting for transfers between devices  5.26 us (4%)
  between operations  1.77 us (1%)
    all_gather x1, blocking collectives, interface_x(): whole = lax.all_gather(packed, 'gx', axis=1, tiled=True)  53.4 us
    all_gather x1, blocking collectives, interface_y(): whole = lax.all_gather(packed, 'gy', axis=1, tiled=True)  13.1 us
    ppermute x2, starting transfers between devices, with_halo(): lax.ppermute(lax.slice_in_dim(block, block.shape[dim] - width, None, axis...  5.74 us
    ppermute x2, waiting for transfers between devices, with_halo(): lax.ppermute(lax.slice_in_dim(block, 0, width, axis=dim), axis, backward)  5.26 us
    sub x24, other arithmetic, eliminate(): right - left_factor * below[3] - right_factor * above[3]  5.16 us
    mul x5, other arithmetic, face_terms(): opened * (0.5 * (flux_a + flux_b) - 0.5 * fastest * (state_b - state_a))  5.04 us
    ppermute x2, starting transfers between devices, with_halo(): lax.ppermute(lax.slice_in_dim(block, 0, width, axis=dim), axis, backward)  4.93 us
    unnamed x53, local copies, waits for them, and re-layouts  4.38 us
  transfers between devices with their start and end apart: 4, of which 2 were waited for; matrix products, arithmetic and copies ran while one was open for 3% of the time, Pallas kernels for 0%

commit v1 on v0

v1 whole, which is shorter than its diff:
```python
import functools

import jax
import jax.numpy as jnp
from jax import lax
from jax.experimental import pallas as pl
from jax.experimental.pallas import tpu as pltpu
from jax.sharding import PartitionSpec as P

MESH = pl.DeviceIdType.MESH
GRAVITY = 9.81
ROOT_G = GRAVITY**0.5
RATIO = 0.05
LANES = 128
TILES = 4
STEPS = 16
TOP = 8
f32 = jnp.float32


def minmod(a, c):
    return jnp.maximum(jnp.minimum(a, c), 0.0) + jnp.minimum(jnp.maximum(a, c), 0.0)


def face_flux(lefts, rights, opened):
    hl, pl_, ql = lefts
    hr, pr, qr = rights
    sl = jnp.where(opened, hl, 1.0)
    sr = jnp.where(opened, hr, 1.0)
    il = lax.rsqrt(sl)
    ir = lax.rsqrt(sr)
    ul = pl_ * (il * il)
    ur = pr * (ir * ir)
    fast = jnp.maximum(
        jnp.abs(ul) + (ROOT_G * sl) * il, jnp.abs(ur) + (ROOT_G * sr) * ir
    )
    factor = jnp.where(opened, 0.5 * RATIO, 0.0)
    mass = (pl_ + pr) - fast * (hr - hl)
    normal = (pl_ * ul + pr * ur) + (0.5 * GRAVITY) * (sl * sl + sr * sr) - fast * (pr - pl_)
    across = (ql * ul + qr * ur) - fast * (qr - ql)
    return factor * mass, factor * normal, factor * across


def lane_up(tiles, lane):
    n = len(tiles)
    rolled = [pltpu.roll(t, LANES - 1, 1) for t in tiles]
    return [jnp.where(lane == LANES - 1, rolled[(i + 1) % n], rolled[i]) for i in range(n)]


def lane_down(tiles, lane):
    n = len(tiles)
    rolled = [pltpu.roll(t, 1, 1) for t in tiles]
    return [jnp.where(lane == 0, rolled[(i - 1) % n], rolled[i]) for i in range(n)]


def matmul2(m, a):
    m11, m12, m21, m22 = m
    a11, a12, a21, a22 = a
    return (
        m11 * a11 + m12 * a21,
        m11 * a12 + m12 * a22,
        m21 * a11 + m22 * a21,
        m21 * a12 + m22 * a22,
    )


def apply2(m, v):
    return (m[0] * v[0] + m[1] * v[1], m[2] * v[0] + m[3] * v[1])


def shifted(values, k, sub, first):
    return tuple(
        jnp.where(sub >= k, pltpu.roll(v, k, 0), f) for v, f in zip(values, first)
    )


IDENT = (1.0, 0.0, 0.0, 1.0)


def scan_matrices(m, sub):
    windows = []
    for k in (1, 2, 4):
        windows.append(m)
        m = matmul2(m, shifted(m, k, sub, IDENT))
    return windows, m, shifted(m, 1, sub, IDENT)


def scan_vectors(windows, v, sub):
    for k, m in zip((1, 2, 4), windows):
        moved = apply2(m, shifted(v, k, sub, (0.0, 0.0)))
        v = (v[0] + moved[0], v[1] + moved[1])
    return v, shifted(v, 1, sub, (0.0, 0.0))


def kernel(
    sizes, spring,
    h_in, p_in, q_in, b_in, m_in,
    corr_out, u_out, v_out,
    fields, wetc, csx, ctr, ax, bx, cx, ay, by, cy, win_x, win_y, pre_x, pre_y,
    faces, qs, qt, vt, os_n, os_u, os_v, pack, got, hc,
    coef_z, coef_x, coef_y, rhs_z, rhs_x, rhs_y, row_y,
    load_sem, halo_send, halo_recv, far_send, far_recv, out_sem,
):
    nx, nz, ny = sizes
    gx = lax.axis_index("gx")
    gy = lax.axis_index("gy")
    xi = lax.div(gx, nz)
    zi = lax.rem(gx, nz)
    ngx = nx * nz

    x_up = (lax.rem(gx + 1, ngx), gy)
    x_dn = (lax.rem(gx + ngx - 1, ngx), gy)
    y_up = (gx, lax.rem(gy + 1, ny))
    y_dn = (gx, lax.rem(gy + ny - 1, ny))
    z_mates = [(xi * nz + lax.rem(zi + k, nz), gy) for k in range(1, nz)]
    x_mates = [(lax.rem(xi + k, nx) * nz + zi, gy) for k in range(1, nx)]
    y_mates = [(gx, lax.rem(gy + k, ny)) for k in range(1, ny)]

    barrier = pltpu.get_barrier_semaphore()
    peers = [x_up, x_dn] + z_mates + x_mates + y_mates
    for peer in peers:
        pl.semaphore_signal(barrier, inc=1, device_id=peer, device_id_type=MESH)

    loads = []
    for i, src in enumerate((h_in, p_in, q_in, b_in, m_in)):
        for l in range(TILES):
            where = pl.ds(l * LANES, LANES)
            dst = fields.at[i, l, pl.ds(TOP, 128), :] if i < 4 else wetc.at[l, pl.ds(TOP, 128), :]
            copy = pltpu.make_async_copy(src.at[:, where], dst, load_sem.at[i * TILES + l])
            copy.start()
            loads.append(copy)

    sub = lax.broadcasted_iota(jnp.int32, (8, LANES), 0)
    lane = lax.broadcasted_iota(jnp.int32, (8, LANES), 1)
    zero = jnp.where(lane + sub < 0, 1.0, 0.0)
    one = jnp.where(lane + sub < 0, 0.0, 1.0)

    def strided(ref, l, start):
        return ref[l, pl.ds(start, 8, stride=STEPS), :]

    def block(t):
        return pl.ds(pl.multiple_of(8 * t, 8), 8)

    for copy in loads[:TILES]:
        copy.wait()

    def start_pieces():
        return tuple((one, zero, zero, one) for _ in range(TILES))

    def coef_step_x(t, carry):
        out = []
        for l in range(TILES):
            ua, ga, ub, gb = carry[l]
            h = fields[0, l, pl.ds(TOP + t, 8, stride=STEPS), :]
            c = spring / (h * h)
            csx[l, block(t), :] = c
            ua = ua + ga
            ub = ub + gb
            ax[l, block(t), :] = ua
            bx[l, block(t), :] = ub
            out.append((ua, ga + c * ua, ub, gb + c * ub))
        return tuple(out)

    ends = lax.fori_loop(0, STEPS, coef_step_x, start_pieces(), unroll=2)
    for l in range(TILES):
        ua, ga, ub, gb = ends[l]
        windows, total, before = scan_matrices((ua, ub, ga, gb), sub)
        for k in range(3):
            for e in range(4):
                win_x[l, 4 * k + e] = windows[k][e]
        for e in range(4):
            pre_x[l, e] = before[e]
        f = 1.0 / total[3]
        coef_x_row = (f, total[1] * f, total[2] * f)
        for e in range(3):
            coef_z[zi, 4 * e + l : 4 * e + l + 1, :] = coef_x_row[e][7:8, :]
            win_x[l, 12 + e] = coef_x_row[e]

    for l in range(TILES):
        ctr[l] = csx[l].T

    def coef_step_y(t, carry):
        out = []
        for l in range(TILES):
            ua, ga, ub, gb = carry[l]
            c = ctr[l, pl.ds(t, 8, stride=STEPS), :]
            ua = ua + ga
            ub = ub + gb
            ay[l, block(t), :] = ua
            by[l, block(t), :] = ub
            out.append((ua, ga + c * ua, ub, gb + c * ub))
        return tuple(out)

    ends = lax.fori_loop(0, STEPS, coef_step_y, start_pieces(), unroll=2)
    total_y = None
    for l in range(TILES):
        ua, ga, ub, gb = ends[l]
        windows, total, before = scan_matrices((ua, ub, ga, gb), sub)
        for k in range(3):
            for e in range(4):
                win_y[l, 4 * k + e] = windows[k][e]
        for e in range(4):
            pre_y[l, e] = before[e]
            win_y[l, 12 + e] = total[e]
        total_y = total if total_y is None else matmul2(total, total_y)
    f = 1.0 / total_y[3]
    coef_y_row = (f, total_y[1] * f, total_y[2] * f)
    for e in range(3):
        coef_y[gy, e : e + 1, :] = coef_y_row[e][7:8, :]
        row_y[e] = coef_y_row[e]

    for copy in loads[TILES:]:
        copy.wait()

    full_lane = lax.broadcasted_iota(jnp.int32, (128, LANES), 1)
    packed = jnp.zeros((128, LANES), f32)
    own = pl.ds(TOP, 128)
    wet_first = wetc[0, own, :].astype(f32)
    wet_last = wetc[TILES - 1, own, :].astype(f32)
    for i in range(3):
        low = fields[i, 0, own, :]
        high = fields[i, TILES - 1, own, :]
        if i:
            low = pltpu.roll(low, 2 * i, 1)
            high = pltpu.roll(high, LANES - 2 * i, 1)
        packed = jnp.where((full_lane >> 1) == i, low, packed)
        packed = jnp.where((full_lane >> 1) == 63 - i, high, packed)
    packed = jnp.where(full_lane == 6, pltpu.roll(fields[3, 0, own, :], 6, 1), packed)
    packed = jnp.where(full_lane == 7, pltpu.roll(wet_first, 7, 1), packed)
    packed = jnp.where(
        full_lane == 121, pltpu.roll(fields[3, TILES - 1, own, :], LANES - 6, 1), packed
    )
    packed = jnp.where(full_lane == 120, pltpu.roll(wet_last, LANES - 7, 1), packed)
    turned = packed.T
    pack[0] = turned[0:8, :]
    pack[1] = turned[120:128, :]

    pl.semaphore_wait(barrier, len(peers))

    def remote(src, dst, send, recv, device):
        copy = pltpu.make_async_remote_copy(
            src_ref=src, dst_ref=dst, send_sem=send, recv_sem=recv,
            device_id=device, device_id_type=MESH,
        )
        copy.start()
        return copy

    halos_x = [
        remote(fields.at[:, :, pl.ds(TOP, 2), :], fields.at[:, :, pl.ds(TOP + 128, 2), :],
               halo_send.at[0], halo_recv.at[0], x_dn),
        remote(fields.at[:, :, pl.ds(TOP + 126, 2), :], fields.at[:, :, pl.ds(TOP - 2, 2), :],
               halo_send.at[1], halo_recv.at[1], x_up),
        remote(wetc.at[:, pl.ds(TOP, 2), :], wetc.at[:, pl.ds(TOP + 128, 2), :],
               halo_send.at[2], halo_recv.at[2], x_dn),
        remote(wetc.at[:, pl.ds(TOP + 126, 2), :], wetc.at[:, pl.ds(TOP - 2, 2), :],
               halo_send.at[3], halo_recv.at[3], x_up),
    ]
    halos_y = [
        remote(pack.at[0], got.at[0], halo_send.at[4], halo_recv.at[4], y_dn),
        remote(pack.at[1], got.at[1], halo_send.at[5], halo_recv.at[5], y_up),
    ]

    def gather(buf, slot, mates, base):
        return [
            remote(buf.at[slot], buf.at[slot], far_send.at[base + i], far_recv.at[base + i], mate)
            for i, mate in enumerate(mates)
        ]

    sent = list(halos_x) + list(halos_y)
    base_y = nz - 1
    base_x = base_y + ny - 1
    half = base_x + nx - 1
    coef_z_copies = gather(coef_z, zi, z_mates, 0)
    coef_y_copies = gather(coef_y, gy, y_mates, base_y)
    sent += coef_z_copies + coef_y_copies

    def x_faces(t):
        for l in range(TILES):
            lefts, rights = [], []
            for i in range(3):
                w = [fields[i, l, pl.ds(TOP + t + d, 8, stride=STEPS), :] for d in (-2, -1, 0, 1)]
                d0 = 0.5 * (w[1] - w[0])
                d1 = 0.5 * (w[2] - w[1])
                d2 = 0.5 * (w[3] - w[2])
                lefts.append(w[1] + minmod(d0, d1))
                rights.append(w[2] - minmod(d1, d2))
            m0 = wetc[l, pl.ds(TOP + t - 1, 8, stride=STEPS), :]
            m1 = wetc[l, pl.ds(TOP + t, 8, stride=STEPS), :]
            flux = face_flux(lefts, rights, (m0 * m1) > 0)
            for i in range(3):
                faces[i, l, block(t), :] = flux[i]

    def interior(t, carry):
        x_faces(t)
        return carry

    lax.fori_loop(2, STEPS - 1, interior, 0)

    for copy in halos_x:
        copy.wait_recv()

    @pl.when(gx == 0)
    def _():
        fields[:, :, TOP - 2 : TOP, :] = jnp.zeros((4, TILES, 2, LANES), f32)
        wetc[:, TOP - 2 : TOP, :] = jnp.zeros((TILES, 2, LANES), jnp.int32)

    @pl.when(gx == ngx - 1)
    def _():
        fields[:, :, TOP + 128 : TOP + 130, :] = jnp.zeros((4, TILES, 2, LANES), f32)
        wetc[:, TOP + 128 : TOP + 130, :] = jnp.zeros((TILES, 2, LANES), jnp.int32)

    def rim(k, carry):
        x_faces(jnp.where(k < 2, k, k + (STEPS - 3)))
        return carry

    lax.fori_loop(0, 4, rim, 0)

    for copy in coef_z_copies:
        copy.wait_recv()

    def port(buf, k):
        return buf[k, 0:4, :], buf[k, 4:8, :], buf[k, 8:12, :]

    group_steps = []
    f, tau, mu = port(coef_z, 0)
    for k in range(1, nz):
        fk, tk, mk = port(coef_z, k)
        inv = 1.0 / (1.0 + tau * mk)
        a = fk * inv
        d = f * inv
        group_steps.append((a, a * tau, d, d * mk))
        f, tau, mu = f * a, tk + fk * (a * tau), mu + f * (d * mk)
    coef_x[xi, 0:4, :] = f
    coef_x[xi, 4:8, :] = tau
    coef_x[xi, 8:12, :] = mu
    coef_x_copies = gather(coef_x, xi, x_mates, base_x)
    sent += coef_x_copies

    for copy in halos_y:
        copy.wait_recv()
    above = jnp.where(gy < ny - 1, got[0], 0.0)
    below = jnp.where(gy > 0, got[1], 0.0)
    hc[...] = jnp.concatenate([above, jnp.zeros((112, LANES), f32), below], axis=0).T

    def y_pass(t, carry):
        edge = hc[pl.ds(t, 8, stride=STEPS), :]

        def rim_tile(up, down):
            return jnp.where(lane < 64, pltpu.roll(edge, LANES - up, 1), pltpu.roll(edge, down, 1))

        rims = [edge, rim_tile(2, 2), rim_tile(4, 4)]
        bed_rim = rim_tile(6, 6)
        wet_rim = rim_tile(7, 7)
        start = pl.ds(TOP + t, 8, stride=STEPS)
        values = [[fields[i, l, start, :] for l in range(TILES)] + [rims[i]] for i in range(3)]
        wet_own = [wetc[l, start, :].astype(f32) for l in range(TILES)]
        wet_all = wet_own + [jnp.where((lane == 0) | (lane == LANES - 1), wet_rim, 0.0)]
        wet_next = lane_up(wet_all, lane)
        opened = [(a * b) > 0.5 for a, b in zip(wet_all, wet_next)]
        lefts, rights = [], []
        for i in (0, 2, 1):
            w = values[i]
            ahead = lane_up(w, lane)
            diff = [0.5 * (a - b) for a, b in zip(ahead, w)]
            before = lane_down(diff, lane)
            slope = [minmod(a, b) for a, b in zip(before, diff)]
            lefts.append([a + s for a, s in zip(w, slope)])
            rights.append(lane_up([a - s for a, s in zip(w, slope)], lane))
        flux = [
            face_flux([x[l] for x in lefts], [x[l] for x in rights], opened[l])
            for l in range(TILES + 1)
        ]
        grads = []
        for i in range(3):
            line = [flux[l][i] for l in range(TILES + 1)]
            past = lane_down(line, lane)
            grads.append([a - b for a, b in zip(line, past)][:TILES])
        bed = [fields[3, l, start, :] for l in range(TILES)] + [bed_rim]
        bed_next = lane_up(bed, lane)
        bed_past = lane_down(bed, lane)
        out = []
        for l in range(TILES):
            uc, gc = carry[l]
            h, p, q = (values[i][l] for i in range(3))
            m = wet_own[l]
            fx = [faces[i, l, block(t + 1), :] - faces[i, l, block(t), :] for i in range(3)]
            push = (0.5 * RATIO * GRAVITY) * h
            bed_up = fields[3, l, pl.ds(TOP + t + 1, 8, stride=STEPS), :]
            bed_dn = fields[3, l, pl.ds(TOP + t - 1, 8, stride=STEPS), :]
            os_n[l, pl.ds(t, 8, stride=STEPS), :] = m * (fx[0] + grads[0][l])
            px = m * (p - fx[1] - grads[2][l] - push * (bed_up - bed_dn))
            qs[l, block(t), :] = m * (
                q - fx[2] - grads[1][l] - push * (bed_next[l] - bed_past[l])
            )
            uc = uc + gc
            cx[l, block(t), :] = uc
            out.append((uc, gc + csx[l, block(t), :] * (uc - px)))
        return tuple(out)

    rest = tuple((zero, zero) for _ in range(TILES))
    ends = lax.fori_loop(0, STEPS, y_pass, rest)

    before_x = []
    for l in range(TILES):
        windows = [[win_x[l, 4 * k + e] for e in range(4)] for k in range(3)]
        total, before = scan_vectors(windows, ends[l], sub)
        before_x.append(before)
        f, tau = win_x[l, 12], win_x[l, 13]
        rhs_z[zi, l : l + 1, :] = (total[0] - tau * total[1])[7:8, :]
        rhs_z[zi, 4 + l : 5 + l, :] = (-(f * total[1]))[7:8, :]
    rhs_z_copies = gather(rhs_z, zi, z_mates, half)
    sent += rhs_z_copies

    outs = [
        pltpu.make_async_copy(os_n.at[l], corr_out.at[:, pl.ds(l * LANES, LANES)], out_sem.at[l])
        for l in range(TILES)
    ]
    for copy in outs:
        copy.start()

    for l in range(TILES):
        qt[l] = qs[l].T

    def rhs_step_y(t, carry):
        out = []
        for l in range(TILES):
            uc, gc = carry[l]
            where = pl.ds(t, 8, stride=STEPS)
            uc = uc + gc
            cy[l, block(t), :] = uc
            out.append((uc, gc + ctr[l, where, :] * (uc - qt[l, where, :])))
        return tuple(out)

    ends = lax.fori_loop(0, STEPS, rhs_step_y, rest, unroll=2)
    before_y, totals_y = [], []
    sum_y = None
    for l in range(TILES):
        windows = [[win_y[l, 4 * k + e] for e in range(4)] for k in range(3)]
        total, before = scan_vectors(windows, ends[l], sub)
        before_y.append(before)
        totals_y.append(total)
        if sum_y is None:
            sum_y = total
        else:
            moved = apply2([win_y[l, 12 + e] for e in range(4)], sum_y)
            sum_y = (total[0] + moved[0], total[1] + moved[1])
    rhs_y[gy, 0:1, :] = (sum_y[0] - row_y[1] * sum_y[1])[7:8, :]
    rhs_y[gy, 1:2, :] = (-(row_y[0] * sum_y[1]))[7:8, :]
    rhs_y_copies = gather(rhs_y, gy, y_mates, half + base_y)
    sent += rhs_y_copies

    def left_chain(ports, mine, rho):
        steps = []
        for k in range(len(ports)):
            fk, tk, mk = ports[k]
            inv = 1.0 / (1.0 + rho * mk)
            a = fk * inv
            steps.append((a, a * rho))
            rho = jnp.where(k < mine, tk + fk * (a * rho), rho)
        return rho, steps

    def right_chain(ports, mine, back):
        steps = [None] * len(ports)
        for k in reversed(range(len(ports))):
            fk, tk, mk = ports[k]
            inv = 1.0 / (1.0 + tk * back)
            a = fk * inv
            steps[k] = (a, a * back)
            back = jnp.where(k >= mine, mk + fk * (a * back), back)
        return back, steps

    def left_values(steps, rhs, mine, w):
        for k in range(len(steps)):
            a, b = steps[k]
            w1, w2 = rhs[k]
            w = jnp.where(k < mine, w1 + a * w + b * w2, w)
        return w

    def right_values(steps, rhs, mine, w):
        for k in reversed(range(len(steps))):
            a, b = steps[k]
            w1, w2 = rhs[k]
            w = jnp.where(k >= mine, w2 + a * w - b * w1, w)
        return w

    def meet(rho, back, wl, wr):
        inv = 1.0 / (1.0 + rho * back)
        return (rho * wr + wl) * inv, (wr - back * wl) * inv

    for copy in coef_y_copies:
        copy.wait_recv()
    ports_y = [tuple(coef_y[k, e : e + 1, :] for e in range(3)) for k in range(ny)]
    row_zero = jnp.zeros((1, LANES), f32)
    rho_y, left_y = left_chain(ports_y, gy, row_zero)
    back_y, right_y = right_chain(ports_y, gy, row_zero + 1.0)

    for copy in coef_x_copies:
        copy.wait_recv()
    ports_x = [port(coef_x, k) for k in range(nx)]
    ports_z = [port(coef_z, k) for k in range(nz)]
    four_zero = jnp.zeros((4, LANES), f32)
    rho_x, left_x = left_chain(ports_x, xi, four_zero)
    back_x, right_x = right_chain(ports_x, xi + 1, four_zero + 1.0)
    rho_z, left_z = left_chain(ports_z, zi, rho_x)
    back_z, right_z = right_chain(ports_z, zi, back_x)

    for copy in rhs_z_copies:
        copy.wait_recv()
    rhs_in_z = [(rhs_z[k, 0:4, :], rhs_z[k, 4:8, :]) for k in range(nz)]
    w1, w2 = rhs_in_z[0]
    for k in range(1, nz):
        a, at, d, dm = group_steps[k - 1]
        k1, k2 = rhs_in_z[k]
        w1, w2 = k1 + a * w1 + at * k2, w2 + d * k2 - dm * w1
    rhs_x[xi, 0:4, :] = w1
    rhs_x[xi, 4:8, :] = w2
    rhs_x_copies = gather(rhs_x, xi, x_mates, half + base_x)
    sent += rhs_x_copies

    for copy in rhs_y_copies:
        copy.wait_recv()
    rhs_in_y = [(rhs_y[k, 0:1, :], rhs_y[k, 1:2, :]) for k in range(ny)]
    wl = left_values(left_y, rhs_in_y, gy, row_zero)
    wr = right_values(right_y, rhs_in_y, gy, row_zero)
    state = meet(rho_y, back_y, wl, wr)
    starts = []
    for l in range(TILES):
        before = [pre_y[l, e] for e in range(4)]
        wide = tuple(jnp.broadcast_to(s, (8, LANES)) for s in state)
        moved = apply2(before, wide)
        starts.append((moved[0] + before_y[l][0], moved[1] + before_y[l][1]))
        if l < TILES - 1:
            moved = apply2([win_y[l, 12 + e] for e in range(4)], wide)
            state = tuple((moved[e] + totals_y[l][e])[7:8, :] for e in range(2))

    def finish_y(t, carry):
        for l in range(TILES):
            at = block(t)
            vt[l, pl.ds(t, 8, stride=STEPS), :] = (
                ay[l, at, :] * starts[l][0] + by[l, at, :] * starts[l][1] + cy[l, at, :]
            )
        return carry

    lax.fori_loop(0, STEPS, finish_y, 0, unroll=2)
    for l in range(TILES):
        natural = vt[l].T
        for t in range(STEPS):
            os_v[l, pl.ds(t, 8, stride=STEPS), :] = natural[8 * t : 8 * t + 8, :]
        copy = pltpu.make_async_copy(
            os_v.at[l], v_out.at[:, pl.ds(l * LANES, LANES)], out_sem.at[TILES + l]
        )
        copy.start()
        outs.append(copy)

    for copy in rhs_x_copies:
        copy.wait_recv()
    rhs_in_x = [(rhs_x[k, 0:4, :], rhs_x[k, 4:8, :]) for k in range(nx)]
    wl = left_values(left_x, rhs_in_x, xi, four_zero)
    wr = right_values(right_x, rhs_in_x, xi + 1, four_zero)
    wl = left_values(left_z, rhs_in_z, zi, wl)
    wr = right_values(right_z, rhs_in_z, zi, wr)
    state = meet(rho_z, back_z, wl, wr)
    for l in range(TILES):
        before = [pre_x[l, e] for e in range(4)]
        wide = tuple(jnp.broadcast_to(s[l : l + 1, :], (8, LANES)) for s in state)
        moved = apply2(before, wide)
        u0, g0 = moved[0] + before_x[l][0], moved[1] + before_x[l][1]
        for t in range(STEPS):
            at = pl.ds(8 * t, 8)
            os_u[l, pl.ds(t, 8, stride=STEPS), :] = (
                ax[l, at, :] * u0 + bx[l, at, :] * g0 + cx[l, at, :]
            )
        copy = pltpu.make_async_copy(
            os_u.at[l], u_out.at[:, pl.ds(l * LANES, LANES)], out_sem.at[2 * TILES + l]
        )
        copy.start()
        outs.append(copy)

    for copy in sent:
        copy.wait_send()
    for copy in outs:
        copy.wait()


def predictor(sizes, spring, depth, momentum_x, momentum_y, bed, wet):
    nx, nz, ny = sizes
    rows, cols = depth.shape
    flat = jax.ShapeDtypeStruct((rows, cols), f32)
    hbm = pl.BlockSpec(memory_space=pl.ANY)
    tile = (TILES, 128, LANES)
    far = 2 * (nz + nx + ny - 3)
    corr, flux_u, flux_v = pl.pallas_call(
        functools.partial(kernel, sizes, spring),
        out_shape=(flat, flat, flat),
        in_specs=[hbm] * 5,
        out_specs=[hbm] * 3,
        scratch_shapes=[
            pltpu.VMEM((4, TILES, 144, LANES), f32),
            pltpu.VMEM((TILES, 144, LANES), jnp.int32),
            pltpu.VMEM(tile, f32),
            pltpu.VMEM(tile, f32),
            pltpu.VMEM(tile, f32),
            pltpu.VMEM(tile, f32),
            pltpu.VMEM(tile, f32),
            pltpu.VMEM(tile, f32),
            pltpu.VMEM(tile, f32),
            pltpu.VMEM(tile, f32),
            pltpu.VMEM((TILES, 16, 8, LANES), f32),
            pltpu.VMEM((TILES, 16, 8, LANES), f32),
            pltpu.VMEM((TILES, 4, 8, LANES), f32),
            pltpu.VMEM((TILES, 4, 8, LANES), f32),
            pltpu.VMEM((3, TILES, 136, LANES), f32),
            pltpu.VMEM(tile, f32),
            pltpu.VMEM(tile, f32),
            pltpu.VMEM(tile, f32),
            pltpu.VMEM(tile, f32),
            pltpu.VMEM(tile, f32),
            pltpu.VMEM(tile, f32),
            pltpu.VMEM((2, 8, LANES), f32),
            pltpu.VMEM((2, 8, LANES), f32),
            pltpu.VMEM((128, LANES), f32),
            pltpu.VMEM((nz, 16, LANES), f32),
            pltpu.VMEM((nx, 16, LANES), f32),
            pltpu.VMEM((ny, 8, LANES), f32),
            pltpu.VMEM((nz, 8, LANES), f32),
            pltpu.VMEM((nx, 8, LANES), f32),
            pltpu.VMEM((ny, 8, LANES), f32),
            pltpu.VMEM((3, 8, LANES), f32),
            pltpu.SemaphoreType.DMA((5 * TILES,)),
            pltpu.SemaphoreType.DMA((6,)),
            pltpu.SemaphoreType.DMA((6,)),
            pltpu.SemaphoreType.DMA((far,)),
            pltpu.SemaphoreType.DMA((far,)),
            pltpu.SemaphoreType.DMA((3 * TILES,)),
        ],
        compiler_params=pltpu.CompilerParams(
            collective_id=0, has_side_effects=True, vmem_limit_bytes=48 * 1024 * 1024
        ),
    )(depth, momentum_x, momentum_y, bed, wet)
    return (depth - corr, flux_u / depth, flux_v / depth)


def solution(mesh):
    ngx, ny = mesh.shape["gx"], mesh.shape["gy"]
    nz = 8 if ngx % 8 == 0 else max(1, ngx // 2)
    sizes = (ngx // nz, nz, ny)
    scale = (4096 / 4.0) ** 2 / 3.0
    place = P("gx", "gy")
    return jax.shard_map(
        functools.partial(predictor, sizes, 1.0 / scale),
        mesh=mesh,
        in_specs=(place,) * 5,
        out_specs=(place,) * 3,
        check_vma=False,
    )
```

time: 122 us -> 36.4 us (0.30)
  blocking collectives: 66.5 us -> 0 us
  Pallas kernels: 0 us -> 29.8 us
  other arithmetic: 28 us -> 0.91 us
  starting transfers between devices: 10.7 us -> 0 us
  waiting for transfers between devices: 5.26 us -> 0 us
  local copies, waits for them, and re-layouts: 9.07 us -> 4.74 us
    all_gather x2 -> x0, blocking collectives: 66.5 us -> none  [the longest x1 53.4 us: interface_x(): whole = lax.all_gather(packed, 'gx', axis=1, tiled=True)]
    pallas_call x0 -> x1, Pallas kernels: none -> 29.8 us  [predictor(): pl.pallas_call(functools.partial(kernel, sizes, spring), out_shape=(flat,...]
    mul x39 -> x0, other arithmetic: 12.6 us -> none  [the longest x5 5.04 us: face_terms(): opened * (0.5 * (flux_a + flux_b) - 0.5 * fastest * (state_b - state_a))]
    ppermute x4 -> x0, starting transfers between devices: 10.7 us -> none  [the longest x2 5.74 us: with_halo(): lax.ppermute(lax.slice_in_dim(block, block.shape[dim] - width, None, axis...]
    sub x42 -> x0, other arithmetic: 8.12 us -> none  [the longest x24 5.16 us: eliminate(): right - left_factor * below[3] - right_factor * above[3]]
    ppermute x4 -> x0, waiting for transfers between devices: 5.26 us -> none  [the longest x2 5.26 us: with_halo(): lax.ppermute(lax.slice_in_dim(block, 0, width, axis=dim), axis, backward)]
    add x6 -> x0, other arithmetic: 2.71 us -> none  [the longest x2 1.28 us: assemble(): inner = solved[0] + solved[1] * prev_wide + solved[2] * own_wide]
    div x6 -> x1, other arithmetic: 2.97 us -> 0.91 us  [predictor(): return (depth - corr, flux_u / depth, flux_v / depth)]
  transfers between devices with their start and end apart: 4 -> 0, of which waited for: 2 -> 0; matrix products, arithmetic and copies ran while one was open for 3% -> 0% of each run, Pallas kernels for 0% -> 0%
where the time goes in v1:
time: 36.4 us; the launch traced here: 36.1 us
  Pallas kernels  29.8 us (82%)
  local copies, waits for them, and re-layouts  4.74 us (13%)
  other arithmetic  0.91 us (2%)
  between operations  0.65 us (2%)
    pallas_call x1, Pallas kernels, predictor(): pl.pallas_call(functools.partial(kernel, sizes, spring), out_shape=(flat,...  29.8 us
    unnamed x10, local copies, waits for them, and re-layouts  4.74 us
    div x1, other arithmetic, predictor(): return (depth - corr, flux_u / depth, flux_v / depth)  0.91 us

profile of v1, /device:TPU:8, one launch (start us, length us, event | category | flops | bytes accessed | tf_op | source)
XLA Modules:
  0.0 36.1 jit_solution(9381816879042048283)
XLA Ops:
  0.6 0.0 copy-start
  0.6 0.9 %copy-done = f32[128,512]{1,0:T(8,128)S(1)} copy-done((f32[128,512]{1,0:T(8,128)S(1)}, f32[128,512]{1,0:T(8,128)}, u32[]{:S(2)}) %copy-start) | copy-done | bytes 262168
  1.6 0.0 copy-start.1
  1.6 0.9 %copy-done.1 = f32[128,512]{1,0:T(8,128)S(1)} copy-done((f32[128,512]{1,0:T(8,128)S(1)}, f32[128,512]{1,0:T(8,128)}, u32[]{:S(2)}) %copy-start.1) | copy-done | bytes 262168
  2.5 0.0 copy-start.2
  2.5 0.9 %copy-done.2 = f32[128,512]{1,0:T(8,128)S(1)} copy-done((f32[128,512]{1,0:T(8,128)S(1)}, f32[128,512]{1,0:T(8,128)}, u32[]{:S(2)}) %copy-start.2) | copy-done | bytes 262168
  3.5 0.0 copy-start.3
  3.5 0.9 %copy-done.3 = f32[128,512]{1,0:T(8,128)S(1)} copy-done((f32[128,512]{1,0:T(8,128)S(1)}, f32[128,512]{1,0:T(8,128)}, u32[]{:S(2)}) %copy-start.3) | copy-done | bytes 262168
  4.4 0.0 copy-start.4
  4.4 0.9 %copy-done.4 = s32[128,512]{1,0:T(8,128)S(1)} copy-done((s32[128,512]{1,0:T(8,128)S(1)}, s32[128,512]{1,0:T(8,128)}, u32[]{:S(2)}) %copy-start.4) | copy-done | bytes 262168
  5.4 29.8 %shard_map.76 = (f32[128,512]{1,0:T(8,128)S(1)}, f32[128,512]{1,0:T(8,128)S(1)}, f32[128,512]{1,0:T(8,128)S(1)}) custom-call(f32[128,512]{1,0:T(8,128)S(1)} %copy-done, f32[128,512]{1,0:T(8,128)S(1)} %copy-done.1, f32[128,512]{1,0:T(8,128)S(1)} %copy-done.2, f32[128,512]{1,0:T(8,128)S(1)} %copy-done.3, s32[128,512]{1,0:T(8,128)S(1)} %copy-done.4), custom_call_target="tpu_custom_call" | custom-call | tf_op jit(solution)/shard_map/pallas_call | solution.py:592
  35.2 0.9 %fusion = (f32[128,512]{1,0:T(8,128)}, f32[128,512]{1,0:T(8,128)}, f32[128,512]{1,0:T(8,128)}) fusion(f32[128,512]{1,0:T(8,128)S(1)} %get-tuple-element.8, f32[128,512]{1,0:T(8,128)S(1)} %copy-done, f32[128,512]{1,0:T(8,128)S(1)} %get-tuple-element.6, f32[128,512]{1,0:T(8,128)S(1)} %get-tuple-element.7), kind=kLoop, calls=%fused_computation | loop fusion | flops 196608 | bytes 1835008 | tf_op jit(solution)/shard_map/div | solution.py:640
Async XLA Ops:
  0.6 1.0 %copy-start = (f32[128,512]{1,0:T(8,128)S(1)}, f32[128,512]{1,0:T(8,128)}, u32[]{:S(2)}) copy-start(f32[128,512]{1,0:T(8,128)} %h_in.1) | copy-start | bytes 786436
  1.6 0.9 %copy-start.1 = (f32[128,512]{1,0:T(8,128)S(1)}, f32[128,512]{1,0:T(8,128)}, u32[]{:S(2)}) copy-start(f32[128,512]{1,0:T(8,128)} %p_in.1) | copy-start | bytes 786436
  2.5 0.9 %copy-start.2 = (f32[128,512]{1,0:T(8,128)S(1)}, f32[128,512]{1,0:T(8,128)}, u32[]{:S(2)}) copy-start(f32[128,512]{1,0:T(8,128)} %q_in.1) | copy-start | bytes 786436
  3.5 0.9 %copy-start.3 = (f32[128,512]{1,0:T(8,128)S(1)}, f32[128,512]{1,0:T(8,128)}, u32[]{:S(2)}) copy-start(f32[128,512]{1,0:T(8,128)} %b_in.1) | copy-start | bytes 786436
  4.4 0.9 %copy-start.4 = (s32[128,512]{1,0:T(8,128)S(1)}, s32[128,512]{1,0:T(8,128)}, u32[]{:S(2)}) copy-start(s32[128,512]{1,0:T(8,128)} %m_in.1) | copy-start | bytes 786436

commit v2 on v1

--- a/solution.py
+++ b/solution.py
@@ -14,7 +14,7 @@
 LANES = 128
 TILES = 4
 STEPS = 16
-TOP = 8
+PITCH = 20
 f32 = jnp.float32
 
 
@@ -96,7 +96,7 @@
     sizes, spring,
     h_in, p_in, q_in, b_in, m_in,
     corr_out, u_out, v_out,
-    fields, wetc, csx, ctr, ax, bx, cx, ay, by, cy, win_x, win_y, pre_x, pre_y,
+    fields, wetc, csx, cty, ax, bx, cx, ay, by, cy, win_x, win_y, pre_x, pre_y,
     faces, qs, qt, vt, os_n, os_u, os_v, pack, got, hc,
     coef_z, coef_x, coef_y, rhs_z, rhs_x, rhs_y, row_y,
     load_sem, halo_send, halo_recv, far_send, far_recv, out_sem,
@@ -123,10 +123,10 @@
 
     loads = []
     for i, src in enumerate((h_in, p_in, q_in, b_in, m_in)):
-        for l in range(TILES):
-            where = pl.ds(l * LANES, LANES)
-            dst = fields.at[i, l, pl.ds(TOP, 128), :] if i < 4 else wetc.at[l, pl.ds(TOP, 128), :]
-            copy = pltpu.make_async_copy(src.at[:, where], dst, load_sem.at[i * TILES + l])
+        for s in range(8):
+            rows = pl.ds(2, STEPS)
+            dst = fields.at[i, rows, s, :] if i < 4 else wetc.at[rows, s, :]
+            copy = pltpu.make_async_copy(src.at[s], dst, load_sem.at[8 * i + s])
             copy.start()
             loads.append(copy)
 
@@ -134,15 +134,69 @@
     lane = lax.broadcasted_iota(jnp.int32, (8, LANES), 1)
     zero = jnp.where(lane + sub < 0, 1.0, 0.0)
     one = jnp.where(lane + sub < 0, 0.0, 1.0)
-
-    def strided(ref, l, start):
-        return ref[l, pl.ds(start, 8, stride=STEPS), :]
+    cols = [pl.ds(LANES * l, LANES) for l in range(TILES)]
 
     def block(t):
         return pl.ds(pl.multiple_of(8 * t, 8), 8)
 
-    for copy in loads[:TILES]:
+    for copy in loads:
         copy.wait()
+
+    full_lane = lax.broadcasted_iota(jnp.int32, (128, LANES), 1)
+
+    def edge(i, l):
+        if i < 4:
+            return fields[i, 2 : 2 + STEPS, :, cols[l]].reshape(128, LANES)
+        return wetc[2 : 2 + STEPS, :, cols[l]].reshape(128, LANES).astype(f32)
+
+    packed = edge(0, 0)
+    packed = jnp.where(full_lane >= 64, edge(0, TILES - 1), packed)
+    for i, width in ((1, 2), (2, 4), (3, 6), (4, 7)):
+        low = pltpu.roll(edge(i, 0), width, 1)
+        high = pltpu.roll(edge(i, TILES - 1), LANES - width, 1)
+        packed = jnp.where((full_lane >= width) & (full_lane < 64), low, packed)
+        packed = jnp.where((full_lane >= 64) & (full_lane < LANES - width), high, packed)
+    turned = packed.T
+    pack[0] = turned[0:8, :]
+    pack[1] = turned[120:128, :]
+
+    pl.semaphore_wait(barrier, len(peers))
+
+    def remote(src, dst, send, recv, device):
+        copy = pltpu.make_async_remote_copy(
+            src_ref=src, dst_ref=dst, send_sem=send, recv_sem=recv,
+            device_id=device, device_id_type=MESH,
+        )
+        copy.start()
+        return copy
+
+    first, last = pl.ds(2, 2), pl.ds(STEPS, 2)
+    past, ahead = pl.ds(0, 2), pl.ds(STEPS + 2, 2)
+    halos_x = [
+        remote(fields.at[:, first, 0, :], fields.at[:, ahead, 7, :],
+               halo_send.at[0], halo_recv.at[0], x_dn),
+        remote(fields.at[:, last, 7, :], fields.at[:, past, 0, :],
+               halo_send.at[1], halo_recv.at[1], x_up),
+        remote(wetc.at[first, 0, :], wetc.at[ahead, 7, :],
+               halo_send.at[2], halo_recv.at[2], x_dn),
+        remote(wetc.at[last, 7, :], wetc.at[past, 0, :],
+               halo_send.at[3], halo_recv.at[3], x_up),
+    ]
+    halos_y = [
+        remote(pack.at[0], got.at[0], halo_send.at[4], halo_recv.at[4], y_dn),
+        remote(pack.at[1], got.at[1], halo_send.at[5], halo_recv.at[5], y_up),
+    ]
+
+    def gather(buf, slot, mates, base):
+        return [
+            remote(buf.at[slot], buf.at[slot], far_send.at[base + i], far_recv.at[base + i], mate)
+            for i, mate in enumerate(mates)
+        ]
+
+    sent = list(halos_x) + list(halos_y)
+    base_y = nz - 1
+    base_x = base_y + ny - 1
+    half = base_x + nx - 1
 
     def start_pieces():
         return tuple((one, zero, zero, one) for _ in range(TILES))
@@ -151,7 +205,7 @@
         out = []
         for l in range(TILES):
             ua, ga, ub, gb = carry[l]
-            h = fields[0, l, pl.ds(TOP + t, 8, stride=STEPS), :]
+            h = fields[0, t + 2, :, cols[l]]
             c = spring / (h * h)
             csx[l, block(t), :] = c
             ua = ua + ga
@@ -175,15 +229,20 @@
         for e in range(3):
             coef_z[zi, 4 * e + l : 4 * e + l + 1, :] = coef_x_row[e][7:8, :]
             win_x[l, 12 + e] = coef_x_row[e]
-
-    for l in range(TILES):
-        ctr[l] = csx[l].T
+    coef_z_copies = gather(coef_z, zi, z_mates, 0)
+
+    def turn(dst, value):
+        for s in range(8):
+            dst[PITCH * s : PITCH * s + STEPS, :] = value[STEPS * s : STEPS * (s + 1), :]
+
+    for l in range(TILES):
+        turn(cty.at[l], csx[l].T)
 
     def coef_step_y(t, carry):
         out = []
         for l in range(TILES):
             ua, ga, ub, gb = carry[l]
-            c = ctr[l, pl.ds(t, 8, stride=STEPS), :]
+            c = cty[l, pl.ds(t, 8, stride=PITCH), :]
             ua = ua + ga
             ub = ub + gb
             ay[l, block(t), :] = ua
@@ -208,112 +267,64 @@
     for e in range(3):
         coef_y[gy, e : e + 1, :] = coef_y_row[e][7:8, :]
         row_y[e] = coef_y_row[e]
-
-    for copy in loads[TILES:]:
-        copy.wait()
-
-    full_lane = lax.broadcasted_iota(jnp.int32, (128, LANES), 1)
-    packed = jnp.zeros((128, LANES), f32)
-    own = pl.ds(TOP, 128)
-    wet_first = wetc[0, own, :].astype(f32)
-    wet_last = wetc[TILES - 1, own, :].astype(f32)
-    for i in range(3):
-        low = fields[i, 0, own, :]
-        high = fields[i, TILES - 1, own, :]
-        if i:
-            low = pltpu.roll(low, 2 * i, 1)
-            high = pltpu.roll(high, LANES - 2 * i, 1)
-        packed = jnp.where((full_lane >> 1) == i, low, packed)
-        packed = jnp.where((full_lane >> 1) == 63 - i, high, packed)
-    packed = jnp.where(full_lane == 6, pltpu.roll(fields[3, 0, own, :], 6, 1), packed)
-    packed = jnp.where(full_lane == 7, pltpu.roll(wet_first, 7, 1), packed)
-    packed = jnp.where(
-        full_lane == 121, pltpu.roll(fields[3, TILES - 1, own, :], LANES - 6, 1), packed
-    )
-    packed = jnp.where(full_lane == 120, pltpu.roll(wet_last, LANES - 7, 1), packed)
-    turned = packed.T
-    pack[0] = turned[0:8, :]
-    pack[1] = turned[120:128, :]
-
-    pl.semaphore_wait(barrier, len(peers))
-
-    def remote(src, dst, send, recv, device):
-        copy = pltpu.make_async_remote_copy(
-            src_ref=src, dst_ref=dst, send_sem=send, recv_sem=recv,
-            device_id=device, device_id_type=MESH,
-        )
-        copy.start()
-        return copy
-
-    halos_x = [
-        remote(fields.at[:, :, pl.ds(TOP, 2), :], fields.at[:, :, pl.ds(TOP + 128, 2), :],
-               halo_send.at[0], halo_recv.at[0], x_dn),
-        remote(fields.at[:, :, pl.ds(TOP + 126, 2), :], fields.at[:, :, pl.ds(TOP - 2, 2), :],
-               halo_send.at[1], halo_recv.at[1], x_up),
-        remote(wetc.at[:, pl.ds(TOP, 2), :], wetc.at[:, pl.ds(TOP + 128, 2), :],
-               halo_send.at[2], halo_recv.at[2], x_dn),
-        remote(wetc.at[:, pl.ds(TOP + 126, 2), :], wetc.at[:, pl.ds(TOP - 2, 2), :],
-               halo_send.at[3], halo_recv.at[3], x_up),
-    ]
-    halos_y = [
-        remote(pack.at[0], got.at[0], halo_send.at[4], halo_recv.at[4], y_dn),
-        remote(pack.at[1], got.at[1], halo_send.at[5], halo_recv.at[5], y_up),
-    ]
-
-    def gather(buf, slot, mates, base):
-        return [
-            remote(buf.at[slot], buf.at[slot], far_send.at[base + i], far_recv.at[base + i], mate)
-            for i, mate in enumerate(mates)
-        ]
-
-    sent = list(halos_x) + list(halos_y)
-    base_y = nz - 1
-    base_x = base_y + ny - 1
-    half = base_x + nx - 1
-    coef_z_copies = gather(coef_z, zi, z_mates, 0)
     coef_y_copies = gather(coef_y, gy, y_mates, base_y)
     sent += coef_z_copies + coef_y_copies
 
-    def x_faces(t):
-        for l in range(TILES):
+    def x_faces(col, dst, start, count):
+        w = [[fields[i, start + d, :, col] for d in range(4)] for i in range(3)]
+        diff = [[0.5 * (w[i][d + 1] - w[i][d]) for d in range(3)] for i in range(3)]
+        slope = [minmod(diff[i][0], diff[i][1]) for i in range(3)]
+        for k in range(count):
             lefts, rights = [], []
             for i in range(3):
-                w = [fields[i, l, pl.ds(TOP + t + d, 8, stride=STEPS), :] for d in (-2, -1, 0, 1)]
-                d0 = 0.5 * (w[1] - w[0])
-                d1 = 0.5 * (w[2] - w[1])
-                d2 = 0.5 * (w[3] - w[2])
-                lefts.append(w[1] + minmod(d0, d1))
-                rights.append(w[2] - minmod(d1, d2))
-            m0 = wetc[l, pl.ds(TOP + t - 1, 8, stride=STEPS), :]
-            m1 = wetc[l, pl.ds(TOP + t, 8, stride=STEPS), :]
+                after = minmod(diff[i][1], diff[i][2])
+                lefts.append(w[i][1] + slope[i])
+                rights.append(w[i][2] - after)
+                slope[i] = after
+                if k + 1 < count:
+                    new = fields[i, start + k + 4, :, col]
+                    w[i] = [None, w[i][2], w[i][3], new]
+                    diff[i] = [None, diff[i][2], 0.5 * (new - w[i][2])]
+            m0 = wetc[start + k + 1, :, col]
+            m1 = wetc[start + k + 2, :, col]
             flux = face_flux(lefts, rights, (m0 * m1) > 0)
             for i in range(3):
-                faces[i, l, block(t), :] = flux[i]
-
-    def interior(t, carry):
-        x_faces(t)
+                faces[i, start + k, :, col] = flux[i]
+
+    def interior(l, carry):
+        x_faces(pl.ds(pl.multiple_of(LANES * l, LANES), LANES), None, 2, STEPS - 3)
         return carry
 
-    lax.fori_loop(2, STEPS - 1, interior, 0)
+    lax.fori_loop(0, TILES, interior, 0)
 
     for copy in halos_x:
         copy.wait_recv()
 
-    @pl.when(gx == 0)
-    def _():
-        fields[:, :, TOP - 2 : TOP, :] = jnp.zeros((4, TILES, 2, LANES), f32)
-        wetc[:, TOP - 2 : TOP, :] = jnp.zeros((TILES, 2, LANES), jnp.int32)
-
-    @pl.when(gx == ngx - 1)
-    def _():
-        fields[:, :, TOP + 128 : TOP + 130, :] = jnp.zeros((4, TILES, 2, LANES), f32)
-        wetc[:, TOP + 128 : TOP + 130, :] = jnp.zeros((TILES, 2, LANES), jnp.int32)
-
-    def rim(k, carry):
-        x_faces(jnp.where(k < 2, k, k + (STEPS - 3)))
+    def fill(ref, kind, both):
+        for l in range(TILES):
+            for t, source, rim, shift in (
+                (0, STEPS, 0, 1), (1, STEPS + 1, 0, 1),
+                (STEPS + 2, 2, 7, 7), (STEPS + 3, 3, 7, 7),
+            ):
+                if not both and t in (0, STEPS + 3):
+                    continue
+                gone = gx == 0 if rim == 0 else gx == ngx - 1
+                border = jnp.where(gone, jnp.zeros((), kind), ref[t, :, cols[l]])
+                ref[t, :, cols[l]] = jnp.where(
+                    sub == rim, border, pltpu.roll(ref[source, :, cols[l]], shift, 0)
+                )
+
+    for i in range(4):
+        fill(fields.at[i], f32, i < 3)
+    fill(wetc, jnp.int32, False)
+
+    def rim_faces(l, carry):
+        col = pl.ds(pl.multiple_of(LANES * l, LANES), LANES)
+        x_faces(col, None, 0, 2)
+        x_faces(col, None, STEPS - 1, 2)
         return carry
 
-    lax.fori_loop(0, 4, rim, 0)
+    lax.fori_loop(0, TILES, rim_faces, 0)
 
     for copy in coef_z_copies:
         copy.wait_recv()
@@ -343,25 +354,24 @@
     hc[...] = jnp.concatenate([above, jnp.zeros((112, LANES), f32), below], axis=0).T
 
     def y_pass(t, carry):
-        edge = hc[pl.ds(t, 8, stride=STEPS), :]
-
-        def rim_tile(up, down):
-            return jnp.where(lane < 64, pltpu.roll(edge, LANES - up, 1), pltpu.roll(edge, down, 1))
-
-        rims = [edge, rim_tile(2, 2), rim_tile(4, 4)]
-        bed_rim = rim_tile(6, 6)
-        wet_rim = rim_tile(7, 7)
-        start = pl.ds(TOP + t, 8, stride=STEPS)
-        values = [[fields[i, l, start, :] for l in range(TILES)] + [rims[i]] for i in range(3)]
-        wet_own = [wetc[l, start, :].astype(f32) for l in range(TILES)]
+        rim = hc[block(t), :]
+
+        def rim_tile(k):
+            return jnp.where(lane < 64, pltpu.roll(rim, LANES - k, 1), pltpu.roll(rim, k, 1))
+
+        rims = [rim, rim_tile(2), rim_tile(4)]
+        bed_rim = rim_tile(6)
+        wet_rim = rim_tile(7)
+        values = [[fields[i, t + 2, :, c] for c in cols] + [rims[i]] for i in range(3)]
+        wet_own = [wetc[t + 2, :, c].astype(f32) for c in cols]
         wet_all = wet_own + [jnp.where((lane == 0) | (lane == LANES - 1), wet_rim, 0.0)]
         wet_next = lane_up(wet_all, lane)
         opened = [(a * b) > 0.5 for a, b in zip(wet_all, wet_next)]
         lefts, rights = [], []
         for i in (0, 2, 1):
             w = values[i]
-            ahead = lane_up(w, lane)
-            diff = [0.5 * (a - b) for a, b in zip(ahead, w)]
+            after = lane_up(w, lane)
+            diff = [0.5 * (a - b) for a, b in zip(after, w)]
             before = lane_down(diff, lane)
             slope = [minmod(a, b) for a, b in zip(before, diff)]
             lefts.append([a + s for a, s in zip(w, slope)])
@@ -373,9 +383,9 @@
         grads = []
         for i in range(3):
             line = [flux[l][i] for l in range(TILES + 1)]
-            past = lane_down(line, lane)
-            grads.append([a - b for a, b in zip(line, past)][:TILES])
-        bed = [fields[3, l, start, :] for l in range(TILES)] + [bed_rim]
+            before = lane_down(line, lane)
+            grads.append([a - b for a, b in zip(line, before)][:TILES])
+        bed = [fields[3, t + 2, :, c] for c in cols] + [bed_rim]
         bed_next = lane_up(bed, lane)
         bed_past = lane_down(bed, lane)
         out = []
@@ -383,12 +393,11 @@
             uc, gc = carry[l]
             h, p, q = (values[i][l] for i in range(3))
             m = wet_own[l]
-            fx = [faces[i, l, block(t + 1), :] - faces[i, l, block(t), :] for i in range(3)]
+            fx = [faces[i, t + 1, :, cols[l]] - faces[i, t, :, cols[l]] for i in range(3)]
             push = (0.5 * RATIO * GRAVITY) * h
-            bed_up = fields[3, l, pl.ds(TOP + t + 1, 8, stride=STEPS), :]
-            bed_dn = fields[3, l, pl.ds(TOP + t - 1, 8, stride=STEPS), :]
-            os_n[l, pl.ds(t, 8, stride=STEPS), :] = m * (fx[0] + grads[0][l])
-            px = m * (p - fx[1] - grads[2][l] - push * (bed_up - bed_dn))
+            os_n[t, :, cols[l]] = m * (fx[0] + grads[0][l])
+            rise = fields[3, t + 3, :, cols[l]] - fields[3, t + 1, :, cols[l]]
+            px = m * (p - fx[1] - grads[2][l] - push * rise)
             qs[l, block(t), :] = m * (
                 q - fx[2] - grads[1][l] - push * (bed_next[l] - bed_past[l])
             )
@@ -411,24 +420,28 @@
     rhs_z_copies = gather(rhs_z, zi, z_mates, half)
     sent += rhs_z_copies
 
-    outs = [
-        pltpu.make_async_copy(os_n.at[l], corr_out.at[:, pl.ds(l * LANES, LANES)], out_sem.at[l])
-        for l in range(TILES)
-    ]
-    for copy in outs:
-        copy.start()
-
-    for l in range(TILES):
-        qt[l] = qs[l].T
+    def store_out(staged, out, base):
+        copies = [
+            pltpu.make_async_copy(staged.at[:, s, :], out.at[s], out_sem.at[base + s])
+            for s in range(8)
+        ]
+        for copy in copies:
+            copy.start()
+        return copies
+
+    outs = store_out(os_n, corr_out, 0)
+
+    for l in range(TILES):
+        turn(qt.at[l], qs[l].T)
 
     def rhs_step_y(t, carry):
         out = []
         for l in range(TILES):
             uc, gc = carry[l]
-            where = pl.ds(t, 8, stride=STEPS)
+            where = pl.ds(t, 8, stride=PITCH)
             uc = uc + gc
             cy[l, block(t), :] = uc
-            out.append((uc, gc + ctr[l, where, :] * (uc - qt[l, where, :])))
+            out.append((uc, gc + cty[l, where, :] * (uc - qt[l, where, :])))
         return tuple(out)
 
     ends = lax.fori_loop(0, STEPS, rhs_step_y, rest, unroll=2)
@@ -536,21 +549,16 @@
     def finish_y(t, carry):
         for l in range(TILES):
             at = block(t)
-            vt[l, pl.ds(t, 8, stride=STEPS), :] = (
+            vt[l, pl.ds(t, 8, stride=PITCH), :] = (
                 ay[l, at, :] * starts[l][0] + by[l, at, :] * starts[l][1] + cy[l, at, :]
             )
         return carry
 
     lax.fori_loop(0, STEPS, finish_y, 0, unroll=2)
     for l in range(TILES):
-        natural = vt[l].T
-        for t in range(STEPS):
-            os_v[l, pl.ds(t, 8, stride=STEPS), :] = natural[8 * t : 8 * t + 8, :]
-        copy = pltpu.make_async_copy(
-            os_v.at[l], v_out.at[:, pl.ds(l * LANES, LANES)], out_sem.at[TILES + l]
-        )
-        copy.start()
-        outs.append(copy)
+        line = [vt[l, PITCH * s : PITCH * s + STEPS, :] for s in range(8)]
+        os_v[:, :, cols[l]] = jnp.concatenate(line, axis=0).T.reshape(STEPS, 8, LANES)
+    outs += store_out(os_v, v_out, 8)
 
     for copy in rhs_x_copies:
         copy.wait_recv()
@@ -567,14 +575,8 @@
         u0, g0 = moved[0] + before_x[l][0], moved[1] + before_x[l][1]
         for t in range(STEPS):
             at = pl.ds(8 * t, 8)
-            os_u[l, pl.ds(t, 8, stride=STEPS), :] = (
-                ax[l, at, :] * u0 + bx[l, at, :] * g0 + cx[l, at, :]
-            )
-        copy = pltpu.make_async_copy(
-            os_u.at[l], u_out.at[:, pl.ds(l * LANES, LANES)], out_sem.at[2 * TILES + l]
-        )
-        copy.start()
-        outs.append(copy)
+            os_u[t, :, cols[l]] = ax[l, at, :] * u0 + bx[l, at, :] * g0 + cx[l, at, :]
+    outs += store_out(os_u, u_out, 16)
 
     for copy in sent:
         copy.wait_send()
@@ -585,20 +587,22 @@
 def predictor(sizes, spring, depth, momentum_x, momentum_y, bed, wet):
     nx, nz, ny = sizes
     rows, cols = depth.shape
-    flat = jax.ShapeDtypeStruct((rows, cols), f32)
+    shape = (8, STEPS, cols)
+    flat = jax.ShapeDtypeStruct(shape, f32)
     hbm = pl.BlockSpec(memory_space=pl.ANY)
     tile = (TILES, 128, LANES)
+    wide = (TILES, 8 * PITCH, LANES)
     far = 2 * (nz + nx + ny - 3)
-    corr, flux_u, flux_v = pl.pallas_call(
+    results = pl.pallas_call(
         functools.partial(kernel, sizes, spring),
         out_shape=(flat, flat, flat),
         in_specs=[hbm] * 5,
         out_specs=[hbm] * 3,
         scratch_shapes=[
-            pltpu.VMEM((4, TILES, 144, LANES), f32),
-            pltpu.VMEM((TILES, 144, LANES), jnp.int32),
-            pltpu.VMEM(tile, f32),
-            pltpu.VMEM(tile, f32),
+            pltpu.VMEM((4, STEPS + 4, 8, cols), f32),
+            pltpu.VMEM((STEPS + 4, 8, cols), jnp.int32),
+            pltpu.VMEM(tile, f32),
+            pltpu.VMEM(wide, f32),
             pltpu.VMEM(tile, f32),
             pltpu.VMEM(tile, f32),
             pltpu.VMEM(tile, f32),
@@ -609,13 +613,13 @@
             pltpu.VMEM((TILES, 16, 8, LANES), f32),
             pltpu.VMEM((TILES, 4, 8, LANES), f32),
             pltpu.VMEM((TILES, 4, 8, LANES), f32),
-            pltpu.VMEM((3, TILES, 136, LANES), f32),
-            pltpu.VMEM(tile, f32),
-            pltpu.VMEM(tile, f32),
-            pltpu.VMEM(tile, f32),
-            pltpu.VMEM(tile, f32),
-            pltpu.VMEM(tile, f32),
-            pltpu.VMEM(tile, f32),
+            pltpu.VMEM((3, STEPS + 1, 8, cols), f32),
+            pltpu.VMEM(tile, f32),
+            pltpu.VMEM(wide, f32),
+            pltpu.VMEM(wide, f32),
+            pltpu.VMEM((STEPS, 8, cols), f32),
+            pltpu.VMEM((STEPS, 8, cols), f32),
+            pltpu.VMEM((STEPS, 8, cols), f32),
             pltpu.VMEM((2, 8, LANES), f32),
             pltpu.VMEM((2, 8, LANES), f32),
             pltpu.VMEM((128, LANES), f32),
@@ -626,17 +630,16 @@
             pltpu.VMEM((nx, 8, LANES), f32),
             pltpu.VMEM((ny, 8, LANES), f32),
             pltpu.VMEM((3, 8, LANES), f32),
-            pltpu.SemaphoreType.DMA((5 * TILES,)),
+            pltpu.SemaphoreType.DMA((40,)),
             pltpu.SemaphoreType.DMA((6,)),
             pltpu.SemaphoreType.DMA((6,)),
             pltpu.SemaphoreType.DMA((far,)),
             pltpu.SemaphoreType.DMA((far,)),
-            pltpu.SemaphoreType.DMA((3 * TILES,)),
+            pltpu.SemaphoreType.DMA((24,)),
         ],
-        compiler_params=pltpu.CompilerParams(
-            collective_id=0, has_side_effects=True, vmem_limit_bytes=48 * 1024 * 1024
-        ),
-    )(depth, momentum_x, momentum_y, bed, wet)
+        compiler_params=pltpu.CompilerParams(collective_id=0, has_side_effects=True),
+    )(*(a.reshape(shape) for a in (depth, momentum_x, momentum_y, bed, wet)))
+    corr, flux_u, flux_v = (a.reshape(rows, cols) for a in results)
     return (depth - corr, flux_u / depth, flux_v / depth)
 
 

time: 36.4 us -> 33.5 us (0.920)
  local copies, waits for them, and re-layouts: 4.74 us -> 0.01 us
  other arithmetic: 0.91 us -> 2.02 us
  Pallas kernels: 29.8 us -> 30.6 us
    unnamed x10 -> x2, local copies, waits for them, and re-layouts: 4.74 us -> 0.01 us
    div x1, other arithmetic: 0.91 us -> 2.02 us  [predictor(): return (depth - corr, flux_u / depth, flux_v / depth)]
    pallas_call x1, Pallas kernels: 29.8 us -> 30.6 us  [predictor(): pl.pallas_call(functools.partial(kernel, sizes, spring), out_shape=(flat,...]
where the time goes in v2:
time: 33.5 us; the launch traced here: 33.3 us
  Pallas kernels  30.6 us (91%)
  other arithmetic  2.02 us (6%)
  between operations  0.66 us (2%)
    pallas_call x1, Pallas kernels, predictor(): pl.pallas_call(functools.partial(kernel, sizes, spring), out_shape=(flat,...  30.6 us
    div x1, other arithmetic, predictor(): return (depth - corr, flux_u / depth, flux_v / depth)  2.02 us

profile of v2, /device:TPU:8, one launch (start us, length us, event | category | flops | bytes accessed | tf_op | source)
XLA Modules:
  0.0 33.3 jit_solution(10951702669424751973)
XLA Ops:
  0.6 0.0 copy-start
  0.6 30.6 %shard_map.76 = (f32[8,16,512]{2,1,0:T(8,128)}, f32[8,16,512]{2,1,0:T(8,128)}, f32[8,16,512]{2,1,0:T(8,128)}) custom-call(f32[8,16,512]{2,1,0:T(8,128)} %bitcast.11, f32[8,16,512]{2,1,0:T(8,128)} %bitcast.12, f32[8,16,512]{2,1,0:T(8,128)} %bitcast.13, f32[8,16,512]{2,1,0:T(8,128)} %bitcast.14, s32[8,16,512]{2,1,0:T(8,128)} %bitcast.15), custom_call_target="tpu_custom_call" | custom-call | tf_op jit(solution)/shard_map/pallas_call | solution.py:596
  31.2 0.0 copy-done
  31.3 2.0 %bitcast_divide_fusion = (f32[128,512]{1,0:T(8,128)}, f32[128,512]{1,0:T(8,128)}, f32[128,512]{1,0:T(8,128)}) fusion(f32[128,512]{1,0:T(8,128)S(1)} %copy-done, f32[8,16,512]{2,1,0:T(8,128)} %get-tuple-element.8, f32[8,16,512]{2,1,0:T(8,128)} %get-tuple-element.6, f32[8,16,512]{2,1,0:T(8,128)} %get-tuple-element.7), kind=kLoop, calls=%fused_computation | loop fusion | flops 196608 | bytes 1835008 | tf_op jit(solution)/shard_map/div | solution.py:643
Async XLA Ops:
  0.6 30.6 %copy-start = (f32[128,512]{1,0:T(8,128)S(1)}, f32[128,512]{1,0:T(8,128)}, u32[]{:S(2)}) copy-start(f32[128,512]{1,0:T(8,128)} %param.5) | copy-start | bytes 786436

commit v3 on v2

--- a/solution.py
+++ b/solution.py
@@ -97,7 +97,7 @@
     h_in, p_in, q_in, b_in, m_in,
     corr_out, u_out, v_out,
     fields, wetc, csx, cty, ax, bx, cx, ay, by, cy, win_x, win_y, pre_x, pre_y,
-    faces, qs, qt, vt, os_n, os_u, os_v, pack, got, hc,
+    faces, qs, qt, vt, os_n, os_u, os_v, ys, edges, got, seq, fix, fixed,
     coef_z, coef_x, coef_y, rhs_z, rhs_x, rhs_y, row_y,
     load_sem, halo_send, halo_recv, far_send, far_recv, out_sem,
 ):
@@ -139,64 +139,8 @@
     def block(t):
         return pl.ds(pl.multiple_of(8 * t, 8), 8)
 
-    for copy in loads:
+    for copy in loads[:8]:
         copy.wait()
-
-    full_lane = lax.broadcasted_iota(jnp.int32, (128, LANES), 1)
-
-    def edge(i, l):
-        if i < 4:
-            return fields[i, 2 : 2 + STEPS, :, cols[l]].reshape(128, LANES)
-        return wetc[2 : 2 + STEPS, :, cols[l]].reshape(128, LANES).astype(f32)
-
-    packed = edge(0, 0)
-    packed = jnp.where(full_lane >= 64, edge(0, TILES - 1), packed)
-    for i, width in ((1, 2), (2, 4), (3, 6), (4, 7)):
-        low = pltpu.roll(edge(i, 0), width, 1)
-        high = pltpu.roll(edge(i, TILES - 1), LANES - width, 1)
-        packed = jnp.where((full_lane >= width) & (full_lane < 64), low, packed)
-        packed = jnp.where((full_lane >= 64) & (full_lane < LANES - width), high, packed)
-    turned = packed.T
-    pack[0] = turned[0:8, :]
-    pack[1] = turned[120:128, :]
-
-    pl.semaphore_wait(barrier, len(peers))
-
-    def remote(src, dst, send, recv, device):
-        copy = pltpu.make_async_remote_copy(
-            src_ref=src, dst_ref=dst, send_sem=send, recv_sem=recv,
-            device_id=device, device_id_type=MESH,
-        )
-        copy.start()
-        return copy
-
-    first, last = pl.ds(2, 2), pl.ds(STEPS, 2)
-    past, ahead = pl.ds(0, 2), pl.ds(STEPS + 2, 2)
-    halos_x = [
-        remote(fields.at[:, first, 0, :], fields.at[:, ahead, 7, :],
-               halo_send.at[0], halo_recv.at[0], x_dn),
-        remote(fields.at[:, last, 7, :], fields.at[:, past, 0, :],
-               halo_send.at[1], halo_recv.at[1], x_up),
-        remote(wetc.at[first, 0, :], wetc.at[ahead, 7, :],
-               halo_send.at[2], halo_recv.at[2], x_dn),
-        remote(wetc.at[last, 7, :], wetc.at[past, 0, :],
-               halo_send.at[3], halo_recv.at[3], x_up),
-    ]
-    halos_y = [
-        remote(pack.at[0], got.at[0], halo_send.at[4], halo_recv.at[4], y_dn),
-        remote(pack.at[1], got.at[1], halo_send.at[5], halo_recv.at[5], y_up),
-    ]
-
-    def gather(buf, slot, mates, base):
-        return [
-            remote(buf.at[slot], buf.at[slot], far_send.at[base + i], far_recv.at[base + i], mate)
-            for i, mate in enumerate(mates)
-        ]
-
-    sent = list(halos_x) + list(halos_y)
-    base_y = nz - 1
-    base_x = base_y + ny - 1
-    half = base_x + nx - 1
 
     def start_pieces():
         return tuple((one, zero, zero, one) for _ in range(TILES))
@@ -229,7 +173,6 @@
         for e in range(3):
             coef_z[zi, 4 * e + l : 4 * e + l + 1, :] = coef_x_row[e][7:8, :]
             win_x[l, 12 + e] = coef_x_row[e]
-    coef_z_copies = gather(coef_z, zi, z_mates, 0)
 
     def turn(dst, value):
         for s in range(8):
@@ -267,6 +210,68 @@
     for e in range(3):
         coef_y[gy, e : e + 1, :] = coef_y_row[e][7:8, :]
         row_y[e] = coef_y_row[e]
+
+    seq[...] = jnp.zeros((5, 24, LANES), f32)
+    fix[...] = jnp.zeros((3, 128, LANES), f32)
+
+    for copy in loads[8:]:
+        copy.wait()
+
+    full_lane = lax.broadcasted_iota(jnp.int32, (128, LANES), 1)
+
+    def edge(i, l):
+        if i < 4:
+            return fields[i, 2 : 2 + STEPS, :, cols[l]].reshape(128, LANES)
+        return wetc[2 : 2 + STEPS, :, cols[l]].reshape(128, LANES).astype(f32)
+
+    packed = jnp.where(full_lane < 64, edge(0, 0), edge(0, TILES - 1))
+    for i in range(1, 5):
+        width = 4 * i
+        low = pltpu.roll(edge(i, 0), width, 1)
+        high = pltpu.roll(edge(i, TILES - 1), LANES - width, 1)
+        packed = jnp.where((full_lane >= width) & (full_lane < 64), low, packed)
+        packed = jnp.where((full_lane >= 64) & (full_lane < LANES - width), high, packed)
+    edges[...] = packed.T
+
+    pl.semaphore_wait(barrier, len(peers))
+
+    def remote(src, dst, send, recv, device):
+        copy = pltpu.make_async_remote_copy(
+            src_ref=src, dst_ref=dst, send_sem=send, recv_sem=recv,
+            device_id=device, device_id_type=MESH,
+        )
+        copy.start()
+        return copy
+
+    first, last = pl.ds(2, 2), pl.ds(STEPS, 2)
+    past, ahead = pl.ds(0, 2), pl.ds(STEPS + 2, 2)
+    halos_x = [
+        remote(fields.at[:, first, 0, :], fields.at[:, ahead, 7, :],
+               halo_send.at[0], halo_recv.at[0], x_dn),
+        remote(fields.at[:, last, 7, :], fields.at[:, past, 0, :],
+               halo_send.at[1], halo_recv.at[1], x_up),
+        remote(wetc.at[first, 0, :], wetc.at[ahead, 7, :],
+               halo_send.at[2], halo_recv.at[2], x_dn),
+        remote(wetc.at[last, 7, :], wetc.at[past, 0, :],
+               halo_send.at[3], halo_recv.at[3], x_up),
+    ]
+    halos_y = [
+        remote(edges.at[pl.ds(0, 24), :], got.at[0], halo_send.at[4], halo_recv.at[4], y_dn),
+        remote(edges.at[pl.ds(104, 24), :], got.at[1], halo_send.at[5], halo_recv.at[5], y_up),
+    ]
+
+    def gather(buf, slot, mates, base):
+        return [
+            remote(buf.at[slot], buf.at[slot], far_send.at[base + i], far_recv.at[base + i], mate)
+            for i, mate in enumerate(mates)
+        ]
+
+    sent = list(halos_x) + list(halos_y)
+    base_y = nz - 1
+    base_x = base_y + ny - 1
+    half = base_x + nx - 1
+
+    coef_z_copies = gather(coef_z, zi, z_mates, 0)
     coef_y_copies = gather(coef_y, gy, y_mates, base_y)
     sent += coef_z_copies + coef_y_copies
 
@@ -297,6 +302,37 @@
 
     lax.fori_loop(0, TILES, interior, 0)
 
+    push_factor = 0.5 * RATIO * GRAVITY
+
+    def y_inner(t, carry):
+        values = [[fields[i, t + 2, :, c] for c in cols] for i in range(3)]
+        wet = [wetc[t + 2, :, c].astype(f32) for c in cols]
+        opened = [(a * b) > 0.5 for a, b in zip(wet, lane_up(wet, lane))]
+        lefts, rights = [], []
+        for i in (0, 2, 1):
+            w = values[i]
+            diff = [0.5 * (a - b) for a, b in zip(lane_up(w, lane), w)]
+            slope = [minmod(a, b) for a, b in zip(lane_down(diff, lane), diff)]
+            lefts.append([a + s for a, s in zip(w, slope)])
+            rights.append(lane_up([a - s for a, s in zip(w, slope)], lane))
+        flux = [
+            face_flux([x[l] for x in lefts], [x[l] for x in rights], opened[l])
+            for l in range(TILES)
+        ]
+        bed = [fields[3, t + 2, :, c] for c in cols]
+        bed_next = lane_up(bed, lane)
+        bed_past = lane_down(bed, lane)
+        for k, i in ((0, 0), (1, 2), (2, 1)):
+            line = [flux[l][i] for l in range(TILES)]
+            for l, before in enumerate(lane_down(line, lane)):
+                grad = line[l] - before
+                if k == 2:
+                    grad = grad + (push_factor * values[0][l]) * (bed_next[l] - bed_past[l])
+                ys[k, t, :, cols[l]] = grad
+        return carry
+
+    lax.fori_loop(0, STEPS, y_inner, 0)
+
     for copy in halos_x:
         copy.wait_recv()
 
@@ -325,6 +361,126 @@
         return carry
 
     lax.fori_loop(0, TILES, rim_faces, 0)
+
+    for copy in halos_y:
+        copy.wait_recv()
+    for i in range(5):
+        low, high = 4 * i, LANES - 4 * i
+        seq[i, 0:2, :] = jnp.where(gy > 0, got[1, 22 - low : 24 - low, :], 0.0)
+        seq[i, 2:6, :] = edges[low : low + 4, :]
+        seq[i, 8:12, :] = edges[high - 4 : high, :]
+        seq[i, 12:14, :] = jnp.where(gy < ny - 1, got[0, low : low + 2, :], 0.0)
+
+    def rows_of(i, d):
+        return seq[i, d : d + 16, :]
+
+    lefts, rights = [], []
+    for i in (0, 2, 1):
+        w = [rows_of(i, d) for d in range(4)]
+        diff = [0.5 * (w[d + 1] - w[d]) for d in range(3)]
+        lefts.append(w[1] + minmod(diff[0], diff[1]))
+        rights.append(w[2] - minmod(diff[1], diff[2]))
+    flux = face_flux(lefts, rights, (rows_of(4, 1) * rows_of(4, 2)) > 0.5)
+    for k, i in ((0, 0), (1, 2), (2, 1)):
+        grad = pltpu.roll(flux[i], 15, 0) - flux[i]
+        if k == 2:
+            grad = grad + (push_factor * rows_of(0, 2)) * (rows_of(3, 3) - rows_of(3, 1))
+        fix[k, 0:2, :] = grad[0:2, :]
+        fix[k, 126:128, :] = grad[8:10, :]
+    for k in (1, 0, 2):
+        fixed[k] = fix[k].T
+
+    def y_grad(k, t, l):
+        grad = ys[k, t, :, cols[l]]
+        if l == 0:
+            return jnp.where(lane < 2, fixed[k, block(t), :], grad)
+        if l == TILES - 1:
+            return jnp.where(lane >= LANES - 2, fixed[k, block(t), :], grad)
+        return grad
+
+    def push_x(t, carry):
+        out = []
+        for l in range(TILES):
+            uc, gc = carry[l]
+            c = cols[l]
+            m = wetc[t + 2, :, c].astype(f32)
+            flow = faces[1, t + 1, :, c] - faces[1, t, :, c]
+            rise = fields[3, t + 3, :, c] - fields[3, t + 1, :, c]
+            px = m * (
+                fields[1, t + 2, :, c] - flow - y_grad(1, t, l)
+                - (push_factor * fields[0, t + 2, :, c]) * rise
+            )
+            uc = uc + gc
+            cx[l, block(t), :] = uc
+            out.append((uc, gc + csx[l, block(t), :] * (uc - px)))
+        return tuple(out)
+
+    rest = tuple((zero, zero) for _ in range(TILES))
+    ends = lax.fori_loop(0, STEPS, push_x, rest, unroll=4)
+
+    before_x = []
+    for l in range(TILES):
+        windows = [[win_x[l, 4 * k + e] for e in range(4)] for k in range(3)]
+        total, before = scan_vectors(windows, ends[l], sub)
+        before_x.append(before)
+        f, tau = win_x[l, 12], win_x[l, 13]
+        rhs_z[zi, l : l + 1, :] = (total[0] - tau * total[1])[7:8, :]
+        rhs_z[zi, 4 + l : 5 + l, :] = (-(f * total[1]))[7:8, :]
+    rhs_z_copies = gather(rhs_z, zi, z_mates, half)
+    sent += rhs_z_copies
+
+    def depth_and_q(t, carry):
+        for l in range(TILES):
+            c = cols[l]
+            m = wetc[t + 2, :, c].astype(f32)
+            os_n[t, :, c] = m * (faces[0, t + 1, :, c] - faces[0, t, :, c] + y_grad(0, t, l))
+            flow = faces[2, t + 1, :, c] - faces[2, t, :, c]
+            qs[l, block(t), :] = m * (fields[2, t + 2, :, c] - flow - y_grad(2, t, l))
+        return carry
+
+    lax.fori_loop(0, STEPS, depth_and_q, 0, unroll=2)
+
+    def store_out(staged, out, base):
+        copies = [
+            pltpu.make_async_copy(staged.at[:, s, :], out.at[s], out_sem.at[base + s])
+            for s in range(8)
+        ]
+        for copy in copies:
+            copy.start()
+        return copies
+
+    outs = store_out(os_n, corr_out, 0)
+
+    for l in range(TILES):
+        turn(qt.at[l], qs[l].T)
+
+    def rhs_step_y(t, carry):
+        out = []
+        for l in range(TILES):
+            uc, gc = carry[l]
+            where = pl.ds(t, 8, stride=PITCH)
+            uc = uc + gc
+            cy[l, block(t), :] = uc
+            out.append((uc, gc + cty[l, where, :] * (uc - qt[l, where, :])))
+        return tuple(out)
+
+    ends = lax.fori_loop(0, STEPS, rhs_step_y, rest, unroll=2)
+    before_y, totals_y = [], []
+    sum_y = None
+    for l in range(TILES):
+        windows = [[win_y[l, 4 * k + e] for e in range(4)] for k in range(3)]
+        total, before = scan_vectors(windows, ends[l], sub)
+        before_y.append(before)
+        totals_y.append(total)
+        if sum_y is None:
+            sum_y = total
+        else:
+            moved = apply2([win_y[l, 12 + e] for e in range(4)], sum_y)
+            sum_y = (total[0] + moved[0], total[1] + moved[1])
+    rhs_y[gy, 0:1, :] = (sum_y[0] - row_y[1] * sum_y[1])[7:8, :]
+    rhs_y[gy, 1:2, :] = (-(row_y[0] * sum_y[1]))[7:8, :]
+    rhs_y_copies = gather(rhs_y, gy, y_mates, half + base_y)
+    sent += rhs_y_copies
 
     for copy in coef_z_copies:
         copy.wait_recv()
@@ -346,121 +502,6 @@
     coef_x[xi, 8:12, :] = mu
     coef_x_copies = gather(coef_x, xi, x_mates, base_x)
     sent += coef_x_copies
-
-    for copy in halos_y:
-        copy.wait_recv()
-    above = jnp.where(gy < ny - 1, got[0], 0.0)
-    below = jnp.where(gy > 0, got[1], 0.0)
-    hc[...] = jnp.concatenate([above, jnp.zeros((112, LANES), f32), below], axis=0).T
-
-    def y_pass(t, carry):
-        rim = hc[block(t), :]
-
-        def rim_tile(k):
-            return jnp.where(lane < 64, pltpu.roll(rim, LANES - k, 1), pltpu.roll(rim, k, 1))
-
-        rims = [rim, rim_tile(2), rim_tile(4)]
-        bed_rim = rim_tile(6)
-        wet_rim = rim_tile(7)
-        values = [[fields[i, t + 2, :, c] for c in cols] + [rims[i]] for i in range(3)]
-        wet_own = [wetc[t + 2, :, c].astype(f32) for c in cols]
-        wet_all = wet_own + [jnp.where((lane == 0) | (lane == LANES - 1), wet_rim, 0.0)]
-        wet_next = lane_up(wet_all, lane)
-        opened = [(a * b) > 0.5 for a, b in zip(wet_all, wet_next)]
-        lefts, rights = [], []
-        for i in (0, 2, 1):
-            w = values[i]
-            after = lane_up(w, lane)
-            diff = [0.5 * (a - b) for a, b in zip(after, w)]
-            before = lane_down(diff, lane)
-            slope = [minmod(a, b) for a, b in zip(before, diff)]
-            lefts.append([a + s for a, s in zip(w, slope)])
-            rights.append(lane_up([a - s for a, s in zip(w, slope)], lane))
-        flux = [
-            face_flux([x[l] for x in lefts], [x[l] for x in rights], opened[l])
-            for l in range(TILES + 1)
-        ]
-        grads = []
-        for i in range(3):
-            line = [flux[l][i] for l in range(TILES + 1)]
-            before = lane_down(line, lane)
-            grads.append([a - b for a, b in zip(line, before)][:TILES])
-        bed = [fields[3, t + 2, :, c] for c in cols] + [bed_rim]
-        bed_next = lane_up(bed, lane)
-        bed_past = lane_down(bed, lane)
-        out = []
-        for l in range(TILES):
-            uc, gc = carry[l]
-            h, p, q = (values[i][l] for i in range(3))
-            m = wet_own[l]
-            fx = [faces[i, t + 1, :, cols[l]] - faces[i, t, :, cols[l]] for i in range(3)]
-            push = (0.5 * RATIO * GRAVITY) * h
-            os_n[t, :, cols[l]] = m * (fx[0] + grads[0][l])
-            rise = fields[3, t + 3, :, cols[l]] - fields[3, t + 1, :, cols[l]]
-            px = m * (p - fx[1] - grads[2][l] - push * rise)
-            qs[l, block(t), :] = m * (
-                q - fx[2] - grads[1][l] - push * (bed_next[l] - bed_past[l])
-            )
-            uc = uc + gc
-            cx[l, block(t), :] = uc
-            out.append((uc, gc + csx[l, block(t), :] * (uc - px)))
-        return tuple(out)
-
-    rest = tuple((zero, zero) for _ in range(TILES))
-    ends = lax.fori_loop(0, STEPS, y_pass, rest)
-
-    before_x = []
-    for l in range(TILES):
-        windows = [[win_x[l, 4 * k + e] for e in range(4)] for k in range(3)]
-        total, before = scan_vectors(windows, ends[l], sub)
-        before_x.append(before)
-        f, tau = win_x[l, 12], win_x[l, 13]
-        rhs_z[zi, l : l + 1, :] = (total[0] - tau * total[1])[7:8, :]
-        rhs_z[zi, 4 + l : 5 + l, :] = (-(f * total[1]))[7:8, :]
-    rhs_z_copies = gather(rhs_z, zi, z_mates, half)
-    sent += rhs_z_copies
-
-    def store_out(staged, out, base):
-        copies = [
-            pltpu.make_async_copy(staged.at[:, s, :], out.at[s], out_sem.at[base + s])
-            for s in range(8)
-        ]
-        for copy in copies:
-            copy.start()
-        return copies
-
-    outs = store_out(os_n, corr_out, 0)
-
-    for l in range(TILES):
-        turn(qt.at[l], qs[l].T)
-
-    def rhs_step_y(t, carry):
-        out = []
-        for l in range(TILES):
-            uc, gc = carry[l]
-            where = pl.ds(t, 8, stride=PITCH)
-            uc = uc + gc
-            cy[l, block(t), :] = uc
-            out.append((uc, gc + cty[l, where, :] * (uc - qt[l, where, :])))
-        return tuple(out)
-
-    ends = lax.fori_loop(0, STEPS, rhs_step_y, rest, unroll=2)
-    before_y, totals_y = [], []
-    sum_y = None
-    for l in range(TILES):
-        windows = [[win_y[l, 4 * k + e] for e in range(4)] for k in range(3)]
-        total, before = scan_vectors(windows, ends[l], sub)
-        before_y.append(before)
-        totals_y.append(total)
-        if sum_y is None:
-            sum_y = total
-        else:
-            moved = apply2([win_y[l, 12 + e] for e in range(4)], sum_y)
-            sum_y = (total[0] + moved[0], total[1] + moved[1])
-    rhs_y[gy, 0:1, :] = (sum_y[0] - row_y[1] * sum_y[1])[7:8, :]
-    rhs_y[gy, 1:2, :] = (-(row_y[0] * sum_y[1]))[7:8, :]
-    rhs_y_copies = gather(rhs_y, gy, y_mates, half + base_y)
-    sent += rhs_y_copies
 
     def left_chain(ports, mine, rho):
         steps = []
@@ -620,9 +661,12 @@
             pltpu.VMEM((STEPS, 8, cols), f32),
             pltpu.VMEM((STEPS, 8, cols), f32),
             pltpu.VMEM((STEPS, 8, cols), f32),
-            pltpu.VMEM((2, 8, LANES), f32),
-            pltpu.VMEM((2, 8, LANES), f32),
+            pltpu.VMEM((3, STEPS, 8, cols), f32),
             pltpu.VMEM((128, LANES), f32),
+            pltpu.VMEM((2, 24, LANES), f32),
+            pltpu.VMEM((5, 24, LANES), f32),
+            pltpu.VMEM((3, 128, LANES), f32),
+            pltpu.VMEM((3, 128, LANES), f32),
             pltpu.VMEM((nz, 16, LANES), f32),
             pltpu.VMEM((nx, 16, LANES), f32),
             pltpu.VMEM((ny, 8, LANES), f32),

time: 33.5 us -> 27.6 us (0.82)
  Pallas kernels: 30.6 us -> 24.5 us
    pallas_call x1, Pallas kernels: 30.6 us -> 24.5 us  [predictor(): pl.pallas_call(functools.partial(kernel, sizes, spring), out_shape=(flat,...]
where the time goes in v3:
time: 27.6 us; the launch traced here: 27.2 us
  Pallas kernels  24.5 us (89%)
  other arithmetic  2.02 us (7%)
  between operations  0.66 us (2%)
    pallas_call x1, Pallas kernels, predictor(): pl.pallas_call(functools.partial(kernel, sizes, spring), out_shape=(flat,...  24.5 us
    div x1, other arithmetic, predictor(): return (depth - corr, flux_u / depth, flux_v / depth)  2.02 us

profile of v3, /device:TPU:8, one launch (start us, length us, event | category | flops | bytes accessed | tf_op | source)
XLA Modules:
  0.0 27.2 jit_solution(12179811339059377991)
XLA Ops:
  0.6 0.0 copy-start
  0.6 24.5 %shard_map.76 = (f32[8,16,512]{2,1,0:T(8,128)}, f32[8,16,512]{2,1,0:T(8,128)}, f32[8,16,512]{2,1,0:T(8,128)}) custom-call(f32[8,16,512]{2,1,0:T(8,128)} %bitcast.11, f32[8,16,512]{2,1,0:T(8,128)} %bitcast.12, f32[8,16,512]{2,1,0:T(8,128)} %bitcast.13, f32[8,16,512]{2,1,0:T(8,128)} %bitcast.14, s32[8,16,512]{2,1,0:T(8,128)} %bitcast.15), custom_call_target="tpu_custom_call" | custom-call | tf_op jit(solution)/shard_map/pallas_call | solution.py:637
  25.2 0.0 copy-done
  25.2 2.0 %bitcast_divide_fusion = (f32[128,512]{1,0:T(8,128)}, f32[128,512]{1,0:T(8,128)}, f32[128,512]{1,0:T(8,128)}) fusion(f32[128,512]{1,0:T(8,128)S(1)} %copy-done, f32[8,16,512]{2,1,0:T(8,128)} %get-tuple-element.8, f32[8,16,512]{2,1,0:T(8,128)} %get-tuple-element.6, f32[8,16,512]{2,1,0:T(8,128)} %get-tuple-element.7), kind=kLoop, calls=%fused_computation | loop fusion | flops 196608 | bytes 1835008 | tf_op jit(solution)/shard_map/div | solution.py:687
Async XLA Ops:
  0.6 24.5 %copy-start = (f32[128,512]{1,0:T(8,128)S(1)}, f32[128,512]{1,0:T(8,128)}, u32[]{:S(2)}) copy-start(f32[128,512]{1,0:T(8,128)} %param.5) | copy-start | bytes 786436

commit v4 on v3

--- a/solution.py
+++ b/solution.py
@@ -681,7 +681,7 @@
             pltpu.SemaphoreType.DMA((far,)),
             pltpu.SemaphoreType.DMA((24,)),
         ],
-        compiler_params=pltpu.CompilerParams(collective_id=0, has_side_effects=True),
+        compiler_params=pltpu.CompilerParams(collective_id=0, has_side_effects=True, vmem_limit_bytes=55_700_000),
     )(*(a.reshape(shape) for a in (depth, momentum_x, momentum_y, bed, wet)))
     corr, flux_u, flux_v = (a.reshape(rows, cols) for a in results)
     return (depth - corr, flux_u / depth, flux_v / depth)

time: 27.6 us -> 26.1 us (0.946)
  other arithmetic: 2.02 us -> 0.92 us
  Pallas kernels: 24.5 us -> 24.1 us
    div x1, other arithmetic: 2.02 us -> 0.92 us  [predictor(): return (depth - corr, flux_u / depth, flux_v / depth)]
    pallas_call x1, Pallas kernels: 24.5 us -> 24.1 us  [predictor(): pl.pallas_call(functools.partial(kernel, sizes, spring), out_shape=(flat,...]
where the time goes in v4:
time: 26.1 us; the launch traced here: 25.7 us
  Pallas kernels  24.1 us (92%)
  other arithmetic  0.92 us (4%)
  between operations  0.66 us (3%)
    pallas_call x1, Pallas kernels, predictor(): pl.pallas_call(functools.partial(kernel, sizes, spring), out_shape=(flat,...  24.1 us
    div x1, other arithmetic, predictor(): return (depth - corr, flux_u / depth, flux_v / depth)  0.92 us

profile of v4, /device:TPU:8, one launch (start us, length us, event | category | flops | bytes accessed | tf_op | source)
XLA Modules:
  0.0 25.7 jit_solution(12086483012487100407)
XLA Ops:
  0.6 0.0 copy-start
  0.6 24.1 %shard_map.76 = (f32[8,16,512]{2,1,0:T(8,128)S(1)}, f32[8,16,512]{2,1,0:T(8,128)S(1)}, f32[8,16,512]{2,1,0:T(8,128)S(1)}) custom-call(f32[8,16,512]{2,1,0:T(8,128)} %bitcast.11, f32[8,16,512]{2,1,0:T(8,128)} %bitcast.12, f32[8,16,512]{2,1,0:T(8,128)} %bitcast.13, f32[8,16,512]{2,1,0:T(8,128)} %bitcast.14, s32[8,16,512]{2,1,0:T(8,128)} %bitcast.15), custom_call_target="tpu_custom_call" | custom-call | tf_op jit(solution)/shard_map/pallas_call | solution.py:637
  24.8 0.0 copy-done
  24.8 0.9 %bitcast_divide_fusion = (f32[128,512]{1,0:T(8,128)}, f32[128,512]{1,0:T(8,128)}, f32[128,512]{1,0:T(8,128)}) fusion(f32[128,512]{1,0:T(8,128)S(1)} %copy-done, f32[8,16,512]{2,1,0:T(8,128)S(1)} %get-tuple-element.8, f32[8,16,512]{2,1,0:T(8,128)S(1)} %get-tuple-element.6, f32[8,16,512]{2,1,0:T(8,128)S(1)} %get-tuple-element.7), kind=kLoop, calls=%fused_computation | loop fusion | flops 196608 | bytes 1835008 | tf_op jit(solution)/shard_map/div | solution.py:687
Async XLA Ops:
  0.6 24.1 %copy-start = (f32[128,512]{1,0:T(8,128)S(1)}, f32[128,512]{1,0:T(8,128)}, u32[]{:S(2)}) copy-start(f32[128,512]{1,0:T(8,128)} %param.5) | copy-start | bytes 786436

commit v5 on v2

v5 whole, which is shorter than its diff:
```python
import functools

import jax
import jax.numpy as jnp
from jax import lax
from jax.experimental import pallas as pl
from jax.experimental.pallas import tpu as pltpu
from jax.sharding import PartitionSpec as P

MESH = pl.DeviceIdType.MESH
GRAVITY = 9.81
ROOT_G = GRAVITY**0.5
RATIO = 0.05
LANES = 128
TILES = 4
STEPS = 16
PITCH = 20
f32 = jnp.float32


def minmod(a, c):
    return jnp.maximum(jnp.minimum(a, c), 0.0) + jnp.minimum(jnp.maximum(a, c), 0.0)


def face_flux(lefts, rights, opened):
    hl, pl_, ql = lefts
    hr, pr, qr = rights
    sl = jnp.where(opened, hl, 1.0)
    sr = jnp.where(opened, hr, 1.0)
    il = lax.rsqrt(sl)
    ir = lax.rsqrt(sr)
    ul = pl_ * (il * il)
    ur = pr * (ir * ir)
    fast = jnp.maximum(
        jnp.abs(ul) + (ROOT_G * sl) * il, jnp.abs(ur) + (ROOT_G * sr) * ir
    )
    factor = jnp.where(opened, 0.5 * RATIO, 0.0)
    mass = (pl_ + pr) - fast * (hr - hl)
    normal = (pl_ * ul + pr * ur) + (0.5 * GRAVITY) * (sl * sl + sr * sr) - fast * (pr - pl_)
    across = (ql * ul + qr * ur) - fast * (qr - ql)
    return factor * mass, factor * normal, factor * across


def lane_up(tiles, lane):
    n = len(tiles)
    rolled = [pltpu.roll(t, LANES - 1, 1) for t in tiles]
    return [jnp.where(lane == LANES - 1, rolled[(i + 1) % n], rolled[i]) for i in range(n)]


def lane_down(tiles, lane):
    n = len(tiles)
    rolled = [pltpu.roll(t, 1, 1) for t in tiles]
    return [jnp.where(lane == 0, rolled[(i - 1) % n], rolled[i]) for i in range(n)]


def matmul2(m, a):
    m11, m12, m21, m22 = m
    a11, a12, a21, a22 = a
    return (
        m11 * a11 + m12 * a21,
        m11 * a12 + m12 * a22,
        m21 * a11 + m22 * a21,
        m21 * a12 + m22 * a22,
    )


def apply2(m, v):
    return (m[0] * v[0] + m[1] * v[1], m[2] * v[0] + m[3] * v[1])


def shifted(values, k, sub, first):
    return tuple(
        jnp.where(sub >= k, pltpu.roll(v, k, 0), f) for v, f in zip(values, first)
    )


IDENT = (1.0, 0.0, 0.0, 1.0)


def scan_matrices(m, sub):
    windows = []
    for k in (1, 2, 4):
        windows.append(m)
        m = matmul2(m, shifted(m, k, sub, IDENT))
    return windows, m, shifted(m, 1, sub, IDENT)


def scan_vectors(windows, v, sub):
    for k, m in zip((1, 2, 4), windows):
        moved = apply2(m, shifted(v, k, sub, (0.0, 0.0)))
        v = (v[0] + moved[0], v[1] + moved[1])
    return v, shifted(v, 1, sub, (0.0, 0.0))


def kernel(
    sizes, spring,
    h_in, p_in, q_in, b_in, m_in,
    corr_out, u_out, v_out,
    fields, wetc, csx, cty, ax, bx, cx, ay, by, cy, win_x, win_y, pre_x, pre_y,
    faces, qs, qt, vt, os_n, os_u, os_v, ys, edges, got, seq, fix, fixed,
    coef_z, coef_x, coef_y, rhs_z, rhs_x, rhs_y, row_y,
    load_sem, halo_send, halo_recv, far_send, far_recv,
):
    nx, nz, ny = sizes
    gx = lax.axis_index("gx")
    gy = lax.axis_index("gy")
    xi = lax.div(gx, nz)
    zi = lax.rem(gx, nz)
    ngx = nx * nz

    x_up = (lax.rem(gx + 1, ngx), gy)
    x_dn = (lax.rem(gx + ngx - 1, ngx), gy)
    y_up = (gx, lax.rem(gy + 1, ny))
    y_dn = (gx, lax.rem(gy + ny - 1, ny))
    z_mates = [(xi * nz + lax.rem(zi + k, nz), gy) for k in range(1, nz)]
    x_mates = [(lax.rem(xi + k, nx) * nz + zi, gy) for k in range(1, nx)]
    y_mates = [(gx, lax.rem(gy + k, ny)) for k in range(1, ny)]

    barrier = pltpu.get_barrier_semaphore()
    far_first = sorted(range(nz - 1), key=lambda k: abs(k + 1 - nz // 2))
    peers = [z_mates[k] for k in far_first] + [x_up, x_dn] + x_mates + y_mates
    for peer in peers:
        pl.semaphore_signal(barrier, inc=1, device_id=peer, device_id_type=MESH)

    def load(i, src):
        copies = []
        for s in range(8):
            rows = pl.ds(2, STEPS)
            dst = fields.at[i, rows, s, :] if i < 4 else wetc.at[rows, s, :]
            copy = pltpu.make_async_copy(src.at[s], dst, load_sem.at[8 * i + s])
            copy.start()
            copies.append(copy)
        return copies

    loads = load(0, h_in)
    for i, src in ((1, p_in), (2, q_in), (3, b_in), (4, m_in)):
        loads += load(i, src)

    sub = lax.broadcasted_iota(jnp.int32, (8, LANES), 0)
    lane = lax.broadcasted_iota(jnp.int32, (8, LANES), 1)
    zero = jnp.where(lane + sub < 0, 1.0, 0.0)
    one = jnp.where(lane + sub < 0, 0.0, 1.0)
    cols = [pl.ds(LANES * l, LANES) for l in range(TILES)]

    def block(t):
        return pl.ds(pl.multiple_of(8 * t, 8), 8)

    for copy in loads[:8]:
        copy.wait()

    def start_pieces():
        return tuple((one, zero, zero, one) for _ in range(TILES))

    def coef_step_x(t, carry):
        out = []
        for l in range(TILES):
            ua, ga, ub, gb = carry[l]
            h = fields[0, t + 2, :, cols[l]]
            c = spring / (h * h)
            csx[l, block(t), :] = c
            ua = ua + ga
            ub = ub + gb
            ax[l, block(t), :] = ua
            bx[l, block(t), :] = ub
            out.append((ua, ga + c * ua, ub, gb + c * ub))
        return tuple(out)

    ends = lax.fori_loop(0, STEPS, coef_step_x, start_pieces(), unroll=2)
    for l in range(TILES):
        ua, ga, ub, gb = ends[l]
        windows, total, before = scan_matrices((ua, ub, ga, gb), sub)
        for k in range(3):
            for e in range(4):
                win_x[l, 4 * k + e] = windows[k][e]
        for e in range(4):
            pre_x[l, e] = before[e]
        f = 1.0 / total[3]
        coef_x_row = (f, total[1] * f, total[2] * f)
        for e in range(3):
            coef_z[zi, 4 * e + l : 4 * e + l + 1, :] = coef_x_row[e][7:8, :]
            win_x[l, 12 + e] = coef_x_row[e]

    seq[...] = jnp.zeros((5, 24, LANES), f32)
    fix[...] = jnp.zeros((3, 128, LANES), f32)

    for copy in loads[8:]:
        copy.wait()

    full_lane = lax.broadcasted_iota(jnp.int32, (128, LANES), 1)

    def edge(i, l):
        if i < 4:
            return fields[i, 2 : 2 + STEPS, :, cols[l]].reshape(128, LANES)
        return wetc[2 : 2 + STEPS, :, cols[l]].reshape(128, LANES).astype(f32)

    packed = None
    for i in range(5):
        both = jnp.where(full_lane < 64, edge(i, 0), edge(i, TILES - 1))
        both = pltpu.roll(both, 8 * i + 4, 1)
        packed = jnp.where(full_lane >= 8 * i, both, packed) if i else both
    edges[...] = packed.T

    pl.semaphore_wait(barrier, len(peers))

    def remote(src, dst, send, recv, device):
        copy = pltpu.make_async_remote_copy(
            src_ref=src, dst_ref=dst, send_sem=send, recv_sem=recv,
            device_id=device, device_id_type=MESH,
        )
        copy.start()
        return copy

    first, last = pl.ds(2, 2), pl.ds(STEPS, 2)
    past, ahead = pl.ds(0, 2), pl.ds(STEPS + 2, 2)
    halos_x = [
        remote(fields.at[:, first, 0, :], fields.at[:, ahead, 7, :],
               halo_send.at[0], halo_recv.at[0], x_dn),
        remote(fields.at[:, last, 7, :], fields.at[:, past, 0, :],
               halo_send.at[1], halo_recv.at[1], x_up),
        remote(wetc.at[first, 0, :], wetc.at[ahead, 7, :],
               halo_send.at[2], halo_recv.at[2], x_dn),
        remote(wetc.at[last, 7, :], wetc.at[past, 0, :],
               halo_send.at[3], halo_recv.at[3], x_up),
    ]
    halos_y = [
        remote(edges.at[pl.ds(0, 40), :], got.at[0], halo_send.at[4], halo_recv.at[4], y_dn),
        remote(edges.at[pl.ds(0, 40), :], got.at[1], halo_send.at[5], halo_recv.at[5], y_up),
    ]

    def gather(buf, slot, mates, base):
        return [
            remote(buf.at[slot], buf.at[slot], far_send.at[base + i], far_recv.at[base + i], mate)
            for i, mate in enumerate(mates)
        ]

    sent = list(halos_x) + list(halos_y)
    base_y = nz - 1
    base_x = base_y + ny - 1
    half = base_x + nx - 1

    coef_z_copies = gather(coef_z, zi, z_mates, 0)
    sent += coef_z_copies

    def x_faces(col, dst, start, count):
        w = [[fields[i, start + d, :, col] for d in range(4)] for i in range(3)]
        diff = [[0.5 * (w[i][d + 1] - w[i][d]) for d in range(3)] for i in range(3)]
        slope = [minmod(diff[i][0], diff[i][1]) for i in range(3)]
        for k in range(count):
            lefts, rights = [], []
            for i in range(3):
                after = minmod(diff[i][1], diff[i][2])
                lefts.append(w[i][1] + slope[i])
                rights.append(w[i][2] - after)
                slope[i] = after
                if k + 1 < count:
                    new = fields[i, start + k + 4, :, col]
                    w[i] = [None, w[i][2], w[i][3], new]
                    diff[i] = [None, diff[i][2], 0.5 * (new - w[i][2])]
            m0 = wetc[start + k + 1, :, col]
            m1 = wetc[start + k + 2, :, col]
            flux = face_flux(lefts, rights, (m0 * m1) > 0)
            for i in range(3):
                faces[i, start + k, :, col] = flux[i]

    def interior(l, carry):
        x_faces(pl.ds(pl.multiple_of(LANES * l, LANES), LANES), None, 2, STEPS - 3)
        return carry

    lax.fori_loop(0, TILES, interior, 0)

    push_factor = 0.5 * RATIO * GRAVITY

    def y_inner(t, carry):
        values = [[fields[i, t + 2, :, c] for c in cols] for i in range(3)]
        signed = [jnp.where(wetc[t + 2, :, c] > 0, h, -h) for c, h in zip(cols, values[0])]
        signed_next = lane_up(signed, lane)
        opened = [jnp.minimum(a, b) > 0.0 for a, b in zip(signed, signed_next)]
        lefts, rights = [], []
        for i in (0, 2, 1):
            w = values[i]
            after = lane_up(w, lane) if i else [jnp.abs(a) for a in signed_next]
            diff = [0.5 * (a - b) for a, b in zip(after, w)]
            slope = [minmod(a, b) for a, b in zip(lane_down(diff, lane), diff)]
            lefts.append([a + s for a, s in zip(w, slope)])
            rights.append(lane_up([a - s for a, s in zip(w, slope)], lane))
        flux = [
            face_flux([x[l] for x in lefts], [x[l] for x in rights], opened[l])
            for l in range(TILES)
        ]
        across = [flux[l][2] for l in range(TILES)]
        for l, before in enumerate(lane_down(across, lane)):
            ys[0, t, :, cols[l]] = flux[l][0]
            ys[1, t, :, cols[l]] = across[l] - before
            ys[2, t, :, cols[l]] = flux[l][1]
        return carry

    lax.fori_loop(0, STEPS, y_inner, 0)

    for copy in halos_y:
        copy.wait_recv()
    for i in range(5):
        high, low = 8 * i, 8 * i + 4
        seq[i, 0:2, :] = jnp.where(gy > 0, got[1, high + 2 : high + 4, :], 0.0)
        seq[i, 2:6, :] = edges[low : low + 4, :]
        seq[i, 8:12, :] = edges[high : high + 4, :]
        seq[i, 12:14, :] = jnp.where(gy < ny - 1, got[0, low : low + 2, :], 0.0)

    def rows_of(i, d):
        return seq[i, d : d + 16, :]

    lefts, rights = [], []
    for i in (0, 2, 1):
        w = [rows_of(i, d) for d in range(4)]
        diff = [0.5 * (w[d + 1] - w[d]) for d in range(3)]
        lefts.append(w[1] + minmod(diff[0], diff[1]))
        rights.append(w[2] - minmod(diff[1], diff[2]))
    flux = face_flux(lefts, rights, (rows_of(4, 1) * rows_of(4, 2)) > 0.5)
    for k, i in ((0, 0), (1, 2), (2, 1)):
        grad = pltpu.roll(flux[i], 15, 0) - flux[i]
        if k == 2:
            grad = grad + (push_factor * rows_of(0, 2)) * (rows_of(3, 3) - rows_of(3, 1))
        fix[k, 0:2, :] = grad[0:2, :]
        fix[k, 126:128, :] = grad[8:10, :]
    for k in (1, 0, 2):
        fixed[k] = fix[k].T

    for copy in halos_x:
        copy.wait_recv()

    def fill(ref, kind, both):
        for l in range(TILES):
            for t, source, rim, shift in (
                (0, STEPS, 0, 1), (1, STEPS + 1, 0, 1),
                (STEPS + 2, 2, 7, 7), (STEPS + 3, 3, 7, 7),
            ):
                if not both and t in (0, STEPS + 3):
                    continue
                gone = gx == 0 if rim == 0 else gx == ngx - 1
                border = jnp.where(gone, jnp.zeros((), kind), ref[t, :, cols[l]])
                ref[t, :, cols[l]] = jnp.where(
                    sub == rim, border, pltpu.roll(ref[source, :, cols[l]], shift, 0)
                )

    for i in range(4):
        fill(fields.at[i], f32, i < 3)
    fill(wetc, jnp.int32, False)

    def rim_faces(l, carry):
        col = pl.ds(pl.multiple_of(LANES * l, LANES), LANES)
        x_faces(col, None, 0, 2)
        x_faces(col, None, STEPS - 1, 2)
        return carry

    lax.fori_loop(0, TILES, rim_faces, 0)

    def patch(k, t, l, grad):
        if l == 0:
            return jnp.where(lane < 2, fixed[k, block(t), :], grad)
        if l == TILES - 1:
            return jnp.where(lane >= LANES - 2, fixed[k, block(t), :], grad)
        return grad

    def push_x(t, carry):
        out = []
        for l in range(TILES):
            uc, gc = carry[l]
            c = cols[l]
            m = wetc[t + 2, :, c].astype(f32)
            flow = faces[1, t + 1, :, c] - faces[1, t, :, c]
            rise = fields[3, t + 3, :, c] - fields[3, t + 1, :, c]
            px = m * (
                fields[1, t + 2, :, c] - flow - patch(1, t, l, ys[1, t, :, c])
                - (push_factor * fields[0, t + 2, :, c]) * rise
            )
            uc = uc + gc
            cx[l, block(t), :] = uc
            out.append((uc, gc + csx[l, block(t), :] * (uc - px)))
        return tuple(out)

    rest = tuple((zero, zero) for _ in range(TILES))
    ends = lax.fori_loop(0, STEPS, push_x, rest, unroll=4)

    before_x = []
    for l in range(TILES):
        windows = [[win_x[l, 4 * k + e] for e in range(4)] for k in range(3)]
        total, before = scan_vectors(windows, ends[l], sub)
        before_x.append(before)
        f, tau = win_x[l, 12], win_x[l, 13]
        rhs_z[zi, l : l + 1, :] = (total[0] - tau * total[1])[7:8, :]
        rhs_z[zi, 4 + l : 5 + l, :] = (-(f * total[1]))[7:8, :]
    rhs_z_copies = gather(rhs_z, zi, z_mates, half)
    sent += rhs_z_copies

    for copy in coef_z_copies:
        copy.wait_recv()

    def port(buf, k):
        return buf[k, 0:4, :], buf[k, 4:8, :], buf[k, 8:12, :]

    group_steps = []
    f, tau, mu = port(coef_z, 0)
    for k in range(1, nz):
        fk, tk, mk = port(coef_z, k)
        inv = 1.0 / (1.0 + tau * mk)
        a = fk * inv
        d = f * inv
        group_steps.append((a, a * tau, d, d * mk))
        f, tau, mu = f * a, tk + fk * (a * tau), mu + f * (d * mk)
    coef_x[xi, 0:4, :] = f
    coef_x[xi, 4:8, :] = tau
    coef_x[xi, 8:12, :] = mu
    coef_x_copies = gather(coef_x, xi, x_mates, base_x)
    sent += coef_x_copies

    def turn(dst, value):
        for s in range(8):
            dst[PITCH * s : PITCH * s + STEPS, :] = value[STEPS * s : STEPS * (s + 1), :]

    for l in range(TILES):
        turn(cty.at[l], csx[l].T)

    def coef_step_y(t, carry):
        out = []
        for l in range(TILES):
            ua, ga, ub, gb = carry[l]
            c = cty[l, pl.ds(t, 8, stride=PITCH), :]
            ua = ua + ga
            ub = ub + gb
            ay[l, block(t), :] = ua
            by[l, block(t), :] = ub
            out.append((ua, ga + c * ua, ub, gb + c * ub))
        return tuple(out)

    ends = lax.fori_loop(0, STEPS, coef_step_y, start_pieces(), unroll=2)
    total_y = None
    for l in range(TILES):
        ua, ga, ub, gb = ends[l]
        windows, total, before = scan_matrices((ua, ub, ga, gb), sub)
        for k in range(3):
            for e in range(4):
                win_y[l, 4 * k + e] = windows[k][e]
        for e in range(4):
            pre_y[l, e] = before[e]
            win_y[l, 12 + e] = total[e]
        total_y = total if total_y is None else matmul2(total, total_y)
    f = 1.0 / total_y[3]
    coef_y_row = (f, total_y[1] * f, total_y[2] * f)
    for e in range(3):
        coef_y[gy, e : e + 1, :] = coef_y_row[e][7:8, :]
        row_y[e] = coef_y_row[e]
    coef_y_copies = gather(coef_y, gy, y_mates, base_y)
    sent += coef_y_copies

    def depth_and_q(t, carry):
        mass, normal, bed = (
            [ref[t + d, :, c] for c in cols] for ref, d in ((ys.at[0], 0), (ys.at[2], 0), (fields.at[3], 2))
        )
        mass_past, normal_past, bed_past = (lane_down(x, lane) for x in (mass, normal, bed))
        bed_next = lane_up(bed, lane)
        for l in range(TILES):
            c = cols[l]
            m = wetc[t + 2, :, c].astype(f32)
            grad = patch(0, t, l, mass[l] - mass_past[l])
            os_n[t, :, c] = m * (faces[0, t + 1, :, c] - faces[0, t, :, c] + grad)
            slope = (push_factor * fields[0, t + 2, :, c]) * (bed_next[l] - bed_past[l])
            grad = patch(2, t, l, normal[l] - normal_past[l] + slope)
            flow = faces[2, t + 1, :, c] - faces[2, t, :, c]
            qs[l, block(t), :] = m * (fields[2, t + 2, :, c] - flow - grad)
        return carry

    lax.fori_loop(0, STEPS, depth_and_q, 0, unroll=2)

    for l in range(TILES):
        turn(qt.at[l], qs[l].T)

    def rhs_step_y(t, carry):
        out = []
        for l in range(TILES):
            uc, gc = carry[l]
            where = pl.ds(t, 8, stride=PITCH)
            uc = uc + gc
            cy[l, block(t), :] = uc
            out.append((uc, gc + cty[l, where, :] * (uc - qt[l, where, :])))
        return tuple(out)

    ends = lax.fori_loop(0, STEPS, rhs_step_y, rest, unroll=2)
    before_y, totals_y = [], []
    sum_y = None
    for l in range(TILES):
        windows = [[win_y[l, 4 * k + e] for e in range(4)] for k in range(3)]
        total, before = scan_vectors(windows, ends[l], sub)
        before_y.append(before)
        totals_y.append(total)
        if sum_y is None:
            sum_y = total
        else:
            moved = apply2([win_y[l, 12 + e] for e in range(4)], sum_y)
            sum_y = (total[0] + moved[0], total[1] + moved[1])
    rhs_y[gy, 0:1, :] = (sum_y[0] - row_y[1] * sum_y[1])[7:8, :]
    rhs_y[gy, 1:2, :] = (-(row_y[0] * sum_y[1]))[7:8, :]
    rhs_y_copies = gather(rhs_y, gy, y_mates, half + base_y)
    sent += rhs_y_copies

    for copy in rhs_z_copies:
        copy.wait_recv()
    rhs_in_z = [(rhs_z[k, 0:4, :], rhs_z[k, 4:8, :]) for k in range(nz)]
    w1, w2 = rhs_in_z[0]
    for k in range(1, nz):
        a, at, d, dm = group_steps[k - 1]
        k1, k2 = rhs_in_z[k]
        w1, w2 = k1 + a * w1 + at * k2, w2 + d * k2 - dm * w1
    rhs_x[xi, 0:4, :] = w1
    rhs_x[xi, 4:8, :] = w2
    rhs_x_copies = gather(rhs_x, xi, x_mates, half + base_x)
    sent += rhs_x_copies

    def left_chain(ports, mine, rho):
        steps = []
        for k in range(len(ports)):
            fk, tk, mk = ports[k]
            inv = 1.0 / (1.0 + rho * mk)
            a = fk * inv
            steps.append((a, a * rho))
            rho = jnp.where(k < mine, tk + fk * (a * rho), rho)
        return rho, steps

    def right_chain(ports, mine, back):
        steps = [None] * len(ports)
        for k in reversed(range(len(ports))):
            fk, tk, mk = ports[k]
            inv = 1.0 / (1.0 + tk * back)
            a = fk * inv
            steps[k] = (a, a * back)
            back = jnp.where(k >= mine, mk + fk * (a * back), back)
        return back, steps

    def left_values(steps, rhs, mine, w):
        for k in range(len(steps)):
            a, b = steps[k]
            w1, w2 = rhs[k]
            w = jnp.where(k < mine, w1 + a * w + b * w2, w)
        return w

    def right_values(steps, rhs, mine, w):
        for k in reversed(range(len(steps))):
            a, b = steps[k]
            w1, w2 = rhs[k]
            w = jnp.where(k >= mine, w2 + a * w - b * w1, w)
        return w

    def meet(rho, back, wl, wr):
        inv = 1.0 / (1.0 + rho * back)
        return (rho * wr + wl) * inv, (wr - back * wl) * inv

    for copy in coef_y_copies:
        copy.wait_recv()
    ports_y = [tuple(coef_y[k, e : e + 1, :] for e in range(3)) for k in range(ny)]
    row_zero = jnp.zeros((1, LANES), f32)
    rho_y, left_y = left_chain(ports_y, gy, row_zero)
    back_y, right_y = right_chain(ports_y, gy, row_zero + 1.0)

    for copy in coef_x_copies:
        copy.wait_recv()
    ports_x = [port(coef_x, k) for k in range(nx)]
    ports_z = [port(coef_z, k) for k in range(nz)]
    four_zero = jnp.zeros((4, LANES), f32)
    rho_x, left_x = left_chain(ports_x, xi, four_zero)
    back_x, right_x = right_chain(ports_x, xi + 1, four_zero + 1.0)
    rho_z, left_z = left_chain(ports_z, zi, rho_x)
    back_z, right_z = right_chain(ports_z, zi, back_x)

    for copy in rhs_y_copies:
        copy.wait_recv()
    rhs_in_y = [(rhs_y[k, 0:1, :], rhs_y[k, 1:2, :]) for k in range(ny)]
    wl = left_values(left_y, rhs_in_y, gy, row_zero)
    wr = right_values(right_y, rhs_in_y, gy, row_zero)
    state = meet(rho_y, back_y, wl, wr)
    starts = []
    for l in range(TILES):
        before = [pre_y[l, e] for e in range(4)]
        wide = tuple(jnp.broadcast_to(s, (8, LANES)) for s in state)
        moved = apply2(before, wide)
        starts.append((moved[0] + before_y[l][0], moved[1] + before_y[l][1]))
        if l < TILES - 1:
            moved = apply2([win_y[l, 12 + e] for e in range(4)], wide)
            state = tuple((moved[e] + totals_y[l][e])[7:8, :] for e in range(2))

    def finish_y(t, carry):
        for l in range(TILES):
            at = block(t)
            vt[l, pl.ds(t, 8, stride=PITCH), :] = (
                ay[l, at, :] * starts[l][0] + by[l, at, :] * starts[l][1] + cy[l, at, :]
            )
        return carry

    lax.fori_loop(0, STEPS, finish_y, 0, unroll=2)
    for l in range(TILES):
        line = [vt[l, PITCH * s : PITCH * s + STEPS, :] for s in range(8)]
        natural = jnp.concatenate(line, axis=0).T
        for t in range(STEPS):
            os_u[l, pl.ds(t, 8, stride=STEPS), :] = natural[8 * t : 8 * t + 8, :]
        v_out[:, cols[l]] = os_u[l]

    for l in range(TILES):
        for t in range(STEPS):
            os_v[l, pl.ds(t, 8, stride=STEPS), :] = os_n[t, :, cols[l]]
        corr_out[:, cols[l]] = os_v[l]

    own_l = left_values(left_z, rhs_in_z, zi, four_zero)
    own_r = right_values(right_z, rhs_in_z, zi, four_zero)
    gain_l = gain_r = four_zero + 1.0
    for k in range(nz):
        gain_l = jnp.where(k < zi, gain_l * left_z[k][0], gain_l)
        gain_r = jnp.where(k >= zi, gain_r * right_z[k][0], gain_r)
    for copy in rhs_x_copies:
        copy.wait_recv()
    rhs_in_x = [(rhs_x[k, 0:4, :], rhs_x[k, 4:8, :]) for k in range(nx)]
    wl = left_values(left_x, rhs_in_x, xi, four_zero)
    wr = right_values(right_x, rhs_in_x, xi + 1, four_zero)
    wl = own_l + gain_l * wl
    wr = own_r + gain_r * wr
    state = meet(rho_z, back_z, wl, wr)
    for l in range(TILES):
        before = [pre_x[l, e] for e in range(4)]
        wide = tuple(jnp.broadcast_to(s[l : l + 1, :], (8, LANES)) for s in state)
        moved = apply2(before, wide)
        u0, g0 = moved[0] + before_x[l][0], moved[1] + before_x[l][1]
        for t in range(STEPS):
            at = pl.ds(8 * t, 8)
            os_u[l, pl.ds(t, 8, stride=STEPS), :] = ax[l, at, :] * u0 + bx[l, at, :] * g0 + cx[l, at, :]
        u_out[:, cols[l]] = os_u[l]

    for copy in sent:
        copy.wait_send()


def predictor(sizes, spring, depth, momentum_x, momentum_y, bed, wet):
    nx, nz, ny = sizes
    rows, cols = depth.shape
    shape = (8, STEPS, cols)
    flat = jax.ShapeDtypeStruct((rows, cols), f32)
    hbm = pl.BlockSpec(memory_space=pl.ANY)
    tile = (TILES, 128, LANES)
    wide = (TILES, 8 * PITCH, LANES)
    far = 2 * (nz + nx + ny - 3)
    results = pl.pallas_call(
        functools.partial(kernel, sizes, spring),
        out_shape=(flat, flat, flat),
        in_specs=[hbm] * 5,
        out_specs=[pl.BlockSpec(memory_space=pltpu.VMEM)] * 3,
        scratch_shapes=[
            pltpu.VMEM((4, STEPS + 4, 8, cols), f32),
            pltpu.VMEM((STEPS + 4, 8, cols), jnp.int32),
            pltpu.VMEM(tile, f32),
            pltpu.VMEM(wide, f32),
            pltpu.VMEM(tile, f32),
            pltpu.VMEM(tile, f32),
            pltpu.VMEM(tile, f32),
            pltpu.VMEM(tile, f32),
            pltpu.VMEM(tile, f32),
            pltpu.VMEM(tile, f32),
            pltpu.VMEM((TILES, 16, 8, LANES), f32),
            pltpu.VMEM((TILES, 16, 8, LANES), f32),
            pltpu.VMEM((TILES, 4, 8, LANES), f32),
            pltpu.VMEM((TILES, 4, 8, LANES), f32),
            pltpu.VMEM((3, STEPS + 1, 8, cols), f32),
            pltpu.VMEM(tile, f32),
            pltpu.VMEM(wide, f32),
            pltpu.VMEM(wide, f32),
            pltpu.VMEM((STEPS, 8, cols), f32),
            pltpu.VMEM(tile, f32),
            pltpu.VMEM(tile, f32),
            pltpu.VMEM((3, STEPS, 8, cols), f32),
            pltpu.VMEM((128, LANES), f32),
            pltpu.VMEM((2, 40, LANES), f32),
            pltpu.VMEM((5, 24, LANES), f32),
            pltpu.VMEM((3, 128, LANES), f32),
            pltpu.VMEM((3, 128, LANES), f32),
            pltpu.VMEM((nz, 16, LANES), f32),
            pltpu.VMEM((nx, 16, LANES), f32),
            pltpu.VMEM((ny, 8, LANES), f32),
            pltpu.VMEM((nz, 8, LANES), f32),
            pltpu.VMEM((nx, 8, LANES), f32),
            pltpu.VMEM((ny, 8, LANES), f32),
            pltpu.VMEM((3, 8, LANES), f32),
            pltpu.SemaphoreType.DMA((40,)),
            pltpu.SemaphoreType.DMA((6,)),
            pltpu.SemaphoreType.DMA((6,)),
            pltpu.SemaphoreType.DMA((far,)),
            pltpu.SemaphoreType.DMA((far,)),
        ],
        compiler_params=pltpu.CompilerParams(collective_id=0, has_side_effects=True, vmem_limit_bytes=55_700_000),
    )(*(a.reshape(shape) for a in (depth, momentum_x, momentum_y, bed, wet)))
    corr, flux_u, flux_v = results
    return (depth - corr, flux_u / depth, flux_v / depth)


def solution(mesh):
    ngx, ny = mesh.shape["gx"], mesh.shape["gy"]
    nz = 8 if ngx % 8 == 0 else max(1, ngx // 2)
    sizes = (ngx // nz, nz, ny)
    scale = (4096 / 4.0) ** 2 / 3.0
    place = P("gx", "gy")
    return jax.shard_map(
        functools.partial(predictor, sizes, 1.0 / scale),
        mesh=mesh,
        in_specs=(place,) * 5,
        out_specs=(place,) * 3,
        check_vma=False,
    )
```

time: 33.5 us -> 25.6 us (0.76)
  Pallas kernels: 30.6 us -> 23.6 us
  other arithmetic: 2.02 us -> 0.91 us
    pallas_call x1, Pallas kernels: 30.6 us -> 23.6 us  [predictor(): pl.pallas_call(functools.partial(kernel, sizes, spring), out_shape=(flat,...]
    div x1, other arithmetic: 2.02 us -> 0.91 us  [predictor(): return (depth - corr, flux_u / depth, flux_v / depth)]
where the time goes in v5:
time: 25.6 us; the launch traced here: 25.2 us
  Pallas kernels  23.6 us (92%)
  other arithmetic  0.91 us (4%)
  between operations  0.66 us (3%)
    pallas_call x1, Pallas kernels, predictor(): pl.pallas_call(functools.partial(kernel, sizes, spring), out_shape=(flat,...  23.6 us
    div x1, other arithmetic, predictor(): return (depth - corr, flux_u / depth, flux_v / depth)  0.91 us

profile of v5, /device:TPU:8, one launch (start us, length us, event | category | flops | bytes accessed | tf_op | source)
XLA Modules:
  0.0 25.2 jit_solution(15671991600426179931)
XLA Ops:
  0.6 0.0 copy-start
  0.6 23.6 %shard_map.76 = (f32[128,512]{1,0:T(8,128)S(1)}, f32[128,512]{1,0:T(8,128)S(1)}, f32[128,512]{1,0:T(8,128)S(1)}) custom-call(f32[8,16,512]{2,1,0:T(8,128)} %bitcast.5, f32[8,16,512]{2,1,0:T(8,128)} %bitcast.6, f32[8,16,512]{2,1,0:T(8,128)} %bitcast.7, f32[8,16,512]{2,1,0:T(8,128)} %bitcast.8, s32[8,16,512]{2,1,0:T(8,128)} %bitcast.9), custom_call_target="tpu_custom_call" | custom-call | tf_op jit(solution)/shard_map/pallas_call | solution.py:646
  24.3 0.0 copy-done
  24.3 0.9 %fusion = (f32[128,512]{1,0:T(8,128)}, f32[128,512]{1,0:T(8,128)}, f32[128,512]{1,0:T(8,128)}) fusion(f32[128,512]{1,0:T(8,128)S(1)} %get-tuple-element.8, f32[128,512]{1,0:T(8,128)S(1)} %copy-done, f32[128,512]{1,0:T(8,128)S(1)} %get-tuple-element.6, f32[128,512]{1,0:T(8,128)S(1)} %get-tuple-element.7), kind=kLoop, calls=%fused_computation | loop fusion | flops 196608 | bytes 1835008 | tf_op jit(solution)/shard_map/div | solution.py:695
Async XLA Ops:
  0.6 23.7 %copy-start = (f32[128,512]{1,0:T(8,128)S(1)}, f32[128,512]{1,0:T(8,128)}, u32[]{:S(2)}) copy-start(f32[128,512]{1,0:T(8,128)} %param.5) | copy-start | bytes 786436

commit v6 on v5

--- a/solution.py
+++ b/solution.py
@@ -294,7 +294,7 @@
             ys[2, t, :, cols[l]] = flux[l][1]
         return carry
 
-    lax.fori_loop(0, STEPS, y_inner, 0)
+    lax.fori_loop(0, STEPS, y_inner, 0, unroll=2)
 
     for copy in halos_y:
         copy.wait_recv()

time: 25.6 us -> 23.8 us (0.930)
  Pallas kernels: 23.6 us -> 21.9 us
    pallas_call x1, Pallas kernels: 23.6 us -> 21.9 us  [predictor(): pl.pallas_call(functools.partial(kernel, sizes, spring), out_shape=(flat,...]
where the time goes in v6:
time: 23.8 us; the launch traced here: 23.4 us
  Pallas kernels  21.9 us (92%)
  other arithmetic  0.91 us (4%)
  between operations  0.66 us (3%)
    pallas_call x1, Pallas kernels, predictor(): pl.pallas_call(functools.partial(kernel, sizes, spring), out_shape=(flat,...  21.9 us
    div x1, other arithmetic, predictor(): return (depth - corr, flux_u / depth, flux_v / depth)  0.91 us

profile of v6, /device:TPU:8, one launch (start us, length us, event | category | flops | bytes accessed | tf_op | source)
XLA Modules:
  0.0 23.4 jit_solution(10194948850893122497)
XLA Ops:
  0.6 0.0 copy-start
  0.6 21.9 %shard_map.76 = (f32[128,512]{1,0:T(8,128)S(1)}, f32[128,512]{1,0:T(8,128)S(1)}, f32[128,512]{1,0:T(8,128)S(1)}) custom-call(f32[8,16,512]{2,1,0:T(8,128)} %bitcast.5, f32[8,16,512]{2,1,0:T(8,128)} %bitcast.6, f32[8,16,512]{2,1,0:T(8,128)} %bitcast.7, f32[8,16,512]{2,1,0:T(8,128)} %bitcast.8, s32[8,16,512]{2,1,0:T(8,128)} %bitcast.9), custom_call_target="tpu_custom_call" | custom-call | tf_op jit(solution)/shard_map/pallas_call | solution.py:646
  22.5 0.0 copy-done
  22.5 0.9 %fusion = (f32[128,512]{1,0:T(8,128)}, f32[128,512]{1,0:T(8,128)}, f32[128,512]{1,0:T(8,128)}) fusion(f32[128,512]{1,0:T(8,128)S(1)} %get-tuple-element.8, f32[128,512]{1,0:T(8,128)S(1)} %copy-done, f32[128,512]{1,0:T(8,128)S(1)} %get-tuple-element.6, f32[128,512]{1,0:T(8,128)S(1)} %get-tuple-element.7), kind=kLoop, calls=%fused_computation | loop fusion | flops 196608 | bytes 1835008 | tf_op jit(solution)/shard_map/div | solution.py:695
Async XLA Ops:
  0.6 21.9 %copy-start = (f32[128,512]{1,0:T(8,128)S(1)}, f32[128,512]{1,0:T(8,128)}, u32[]{:S(2)}) copy-start(f32[128,512]{1,0:T(8,128)} %param.5) | copy-start | bytes 786436

commit v7 on v6

--- a/solution.py
+++ b/solution.py
@@ -165,7 +165,7 @@
             out.append((ua, ga + c * ua, ub, gb + c * ub))
         return tuple(out)
 
-    ends = lax.fori_loop(0, STEPS, coef_step_x, start_pieces(), unroll=2)
+    ends = lax.fori_loop(0, STEPS, coef_step_x, start_pieces(), unroll=8)
     for l in range(TILES):
         ua, ga, ub, gb = ends[l]
         windows, total, before = scan_matrices((ua, ub, ga, gb), sub)
@@ -266,7 +266,7 @@
         x_faces(pl.ds(pl.multiple_of(LANES * l, LANES), LANES), None, 2, STEPS - 3)
         return carry
 
-    lax.fori_loop(0, TILES, interior, 0)
+    lax.fori_loop(0, TILES, interior, 0, unroll=2)
 
     push_factor = 0.5 * RATIO * GRAVITY
 
@@ -351,7 +351,7 @@
         x_faces(col, None, STEPS - 1, 2)
         return carry
 
-    lax.fori_loop(0, TILES, rim_faces, 0)
+    lax.fori_loop(0, TILES, rim_faces, 0, unroll=2)
 
     def patch(k, t, l, grad):
         if l == 0:
@@ -378,7 +378,7 @@
         return tuple(out)
 
     rest = tuple((zero, zero) for _ in range(TILES))
-    ends = lax.fori_loop(0, STEPS, push_x, rest, unroll=4)
+    ends = lax.fori_loop(0, STEPS, push_x, rest, unroll=8)
 
     before_x = []
     for l in range(TILES):
@@ -431,7 +431,7 @@
             out.append((ua, ga + c * ua, ub, gb + c * ub))
         return tuple(out)
 
-    ends = lax.fori_loop(0, STEPS, coef_step_y, start_pieces(), unroll=2)
+    ends = lax.fori_loop(0, STEPS, coef_step_y, start_pieces(), unroll=4)
     total_y = None
     for l in range(TILES):
         ua, ga, ub, gb = ends[l]
@@ -483,7 +483,7 @@
             out.append((uc, gc + cty[l, where, :] * (uc - qt[l, where, :])))
         return tuple(out)
 
-    ends = lax.fori_loop(0, STEPS, rhs_step_y, rest, unroll=2)
+    ends = lax.fori_loop(0, STEPS, rhs_step_y, rest, unroll=4)
     before_y, totals_y = [], []
     sum_y = None
     for l in range(TILES):
@@ -593,7 +593,7 @@
             )
         return carry
 
-    lax.fori_loop(0, STEPS, finish_y, 0, unroll=2)
+    lax.fori_loop(0, STEPS, finish_y, 0, unroll=4)
     for l in range(TILES):
         line = [vt[l, PITCH * s : PITCH * s + STEPS, :] for s in range(8)]
         natural = jnp.concatenate(line, axis=0).T

time: 23.8 us -> 23.8 us (level)
  no operation moved by 1% of the time
where the time goes in v7:
time: 23.8 us; the launch traced here: 23.4 us
  Pallas kernels  21.8 us (92%)
  other arithmetic  0.91 us (4%)
  between operations  0.66 us (3%)
    pallas_call x1, Pallas kernels, predictor(): pl.pallas_call(functools.partial(kernel, sizes, spring), out_shape=(flat,...  21.8 us
    div x1, other arithmetic, predictor(): return (depth - corr, flux_u / depth, flux_v / depth)  0.91 us

profile of v7, /device:TPU:8, one launch (start us, length us, event | category | flops | bytes accessed | tf_op | source)
XLA Modules:
  0.0 23.4 jit_solution(18399988164563259745)
XLA Ops:
  0.6 0.0 copy-start
  0.6 21.8 %shard_map.76 = (f32[128,512]{1,0:T(8,128)S(1)}, f32[128,512]{1,0:T(8,128)S(1)}, f32[128,512]{1,0:T(8,128)S(1)}) custom-call(f32[8,16,512]{2,1,0:T(8,128)} %bitcast.5, f32[8,16,512]{2,1,0:T(8,128)} %bitcast.6, f32[8,16,512]{2,1,0:T(8,128)} %bitcast.7, f32[8,16,512]{2,1,0:T(8,128)} %bitcast.8, s32[8,16,512]{2,1,0:T(8,128)} %bitcast.9), custom_call_target="tpu_custom_call" | custom-call | tf_op jit(solution)/shard_map/pallas_call | solution.py:646
  22.5 0.0 copy-done
  22.5 0.9 %fusion = (f32[128,512]{1,0:T(8,128)}, f32[128,512]{1,0:T(8,128)}, f32[128,512]{1,0:T(8,128)}) fusion(f32[128,512]{1,0:T(8,128)S(1)} %get-tuple-element.8, f32[128,512]{1,0:T(8,128)S(1)} %copy-done, f32[128,512]{1,0:T(8,128)S(1)} %get-tuple-element.6, f32[128,512]{1,0:T(8,128)S(1)} %get-tuple-element.7), kind=kLoop, calls=%fused_computation | loop fusion | flops 196608 | bytes 1835008 | tf_op jit(solution)/shard_map/div | solution.py:695
Async XLA Ops:
  0.6 21.8 %copy-start = (f32[128,512]{1,0:T(8,128)S(1)}, f32[128,512]{1,0:T(8,128)}, u32[]{:S(2)}) copy-start(f32[128,512]{1,0:T(8,128)} %param.5) | copy-start | bytes 786436
